TPU v7x, 32 devices: a whole 2x2x4 slice. The times are simulated.
32 devices in a mesh: ctx: 16 (over z, x, core), wa: 2 (over y).
Axes of the slice: x: 2, y: 2, z: 4, core: 2. Of those that a mesh axis runs over, the one named last changes fastest.
Arguments:
- hidden_in: bfloat16 [2, 2048, 1024], P('wa', 'ctx')
- out_grad: bfloat16 [2, 2048, 1024], P('wa', 'ctx'), may hold values from -6 to 6
- lengths: int32 [2, 8], P('wa'), may hold values from 1 to 1024, 1792 in all within a row
- permutation: int32 [2, 2048], P('wa'), may hold values from 0 to 2047, each once within a row
- routes: int32 [2, 2048, 2], P('wa', 'ctx'), may hold values from 0 to 7, all different within a row; in each aligned block of 128 rows (0 to 127, 128 to 255, ..., all dimensions but the last counted through in order) at most 64 rows name the same one
- bucket_table: int32 [1024], replicated, may hold values from 0 to 31, never falling along the last dimension, each value on 1 to 256 neighbouring positions
- w_qkv: bfloat16 [1024, 3072], P('wa'), may hold values from -0.1875 to 0.1875
- w_out: bfloat16 [1024, 1024], P('wa'), may hold values from -0.75 to 0.75
- w_in: bfloat16 [16, 1024, 2816], P('ctx', 'wa'), may hold values from -0.1875 to 0.1875
- w_down: bfloat16 [16, 1024, 1408], P('ctx', 'wa'), may hold values from -0.109375 to 0.109375
- w_router: float32 [1024, 8], replicated, may hold values from -0.125 to 0.125
- gain_attn: float32 [1024], replicated, may hold values from 0.5 to 1.5
- gain_moe: float32 [1024], replicated, may hold values from 0.5 to 1.5
- rel_bias: float32 [32, 16], replicated, may hold values from -4 to 4
Outputs:
- block_out: bfloat16 [2, 2048, 1024], P('wa', 'ctx')
- hidden_grad: bfloat16 [2, 2048, 1024], P('wa', 'ctx')
- qkv_grad: float32 [1024, 3072], P('wa')
- out_proj_grad: float32 [1024, 1024], P('wa')
- expert_in_grad: float32 [16, 1024, 2816], P('ctx', 'wa')
- expert_down_grad: float32 [16, 1024, 1408], P('ctx', 'wa')
- router_grad: float32 [1024, 8], replicated
- gain_attn_grad: float32 [1024], replicated
- gain_moe_grad: float32 [1024], replicated
- rel_bias_grad: float32 [32, 16], replicated
- stats: float32 [3], replicated
Inputs may be any that keep to these rules, and one draw needn't show every extreme that they name: In every batch the lengths sum to 1792 and the largest is exactly 1024; sequences lie in order from stream position 0, the rest is padding. Every row is a permutation of the 2048 stream positions of its batch. `routes`: each token names two different experts. Among the 128 slots of one device no expert is named more than 64 times, and on some device some expert is named exactly 64 times. `bucket_table`: never falls as the distance grows; every bucket appears, for at most 256 distances.
All inputs are finite; a program needn't handle non-finite values.
Results may differ from a plain program's by a relative error of at most 0.034.
Values may be sent and summed in bfloat16 or wider, within the bound.
No kernel may reach another device: no remote copies, remote signals or barrier semaphores. Data moves between devices by JAX's collectives and lax.ppermute only.
A program may use at most 192 MiB of HBM per device.

v0:
```python
import math

import jax
import jax.numpy as jnp
from jax import lax
from jax.sharding import PartitionSpec as P

NSEQ = 8


NORM_EPSILON = 1e-06
MASKED_SCORE = -1e30
TOP_PRECISION = lax.Precision.HIGHEST


def rms_norm(features, scale_gain):
    return (
        features
        * lax.rsqrt(jnp.mean(features * features, axis=-1, keepdims=True) + NORM_EPSILON)
        * scale_gain
    )


def glu_act(gate_up):
    middle = gate_up.shape[-1] // 2
    return jax.nn.gelu(gate_up[..., :middle], approximate=True) * gate_up[..., middle:]


def segment_of(positions, bounds):
    return jnp.sum((positions[:, None] >= bounds[None, :]).astype(jnp.int32), axis=1)


def lead_dot(left, right, precision=None):
    return lax.dot_general(
        left,
        right,
        (((0,), (0,)), ((), ())),
        precision=precision,
        preferred_element_type=jnp.float32,
    )


def tail_dot(left, right):
    return lax.dot_general(
        left, right, (((1,), (1,)), ((), ())), preferred_element_type=jnp.float32
    )


def pair_scores(
    queries, key_rows, query_pos, query_seg, key_pos, key_seg, bucket_starts, bias_table
):
    bucket_count = bias_table.shape[0]
    raw_scores = jnp.einsum("qhd,khd->hqk", queries, key_rows, preferred_element_type=jnp.float32)
    distance = query_pos[:, None] - key_pos[None, :]
    clipped = jnp.maximum(distance, 0)
    bucket_ids = jnp.sum(
        (clipped[:, :, None] >= bucket_starts[None, None, 1:]).astype(jnp.int32), axis=2
    )
    bucket_hot = (
        bucket_ids[:, :, None] == jnp.arange(bucket_count, dtype=jnp.int32)[None, None, :]
    ).astype(jnp.float32)
    bias_block = jnp.einsum("qkb,bh->hqk", bucket_hot, bias_table, precision=TOP_PRECISION)
    scores = raw_scores * 0.125 + bias_block
    allowed = (
        (query_seg[:, None] == key_seg[None, :]) & (distance >= 0) & (query_seg[:, None] < NSEQ)
    )
    return (scores, allowed, bucket_hot)


def attend_piece(
    running, pieces, queries, query_pos, query_seg, perm_row, bounds, bucket_starts, bias_table
):
    key_rows, value_rows = pieces
    piece_rows = key_rows.shape[0]
    head_count = queries.shape[1]
    block_rows = math.gcd(piece_rows, 512)
    keys_split = key_rows.reshape(piece_rows, head_count, -1)
    values_split = value_rows.reshape(piece_rows, head_count, -1)

    def step(step_index, state):
        row_max, totals, weighted = state
        offset = step_index * block_rows
        key_block = lax.dynamic_slice_in_dim(keys_split, offset, block_rows, 0)
        value_block = lax.dynamic_slice_in_dim(values_split, offset, block_rows, 0)
        key_pos = lax.dynamic_slice_in_dim(perm_row, offset, block_rows, 0)
        key_seg = segment_of(key_pos, bounds)
        scores, allowed, _ = pair_scores(
            queries, key_block, query_pos, query_seg, key_pos, key_seg, bucket_starts, bias_table
        )
        new_max = jnp.maximum(row_max, jnp.max(jnp.where(allowed, scores, MASKED_SCORE), axis=2))
        factor = jnp.exp(row_max - new_max)
        exp_scores = jnp.exp(jnp.where(allowed, scores - new_max[:, :, None], MASKED_SCORE))
        totals = totals * factor + jnp.sum(exp_scores, axis=2)
        weighted = weighted * factor[:, :, None] + jnp.einsum(
            "hqk,khd->hqd",
            exp_scores.astype(jnp.bfloat16),
            value_block,
            preferred_element_type=jnp.float32,
        )
        return (new_max, totals, weighted)

    return lax.fori_loop(0, piece_rows // block_rows, step, running)


def block_grads(
    queries,
    dout_low,
    log_total,
    row_delta,
    query_pos,
    query_seg,
    key_block,
    value_block,
    key_pos,
    key_seg,
    bucket_starts,
    bias_table,
):
    scores, allowed, bucket_hot = pair_scores(
        queries, key_block, query_pos, query_seg, key_pos, key_seg, bucket_starts, bias_table
    )
    attn_probs = jnp.exp(jnp.where(allowed, scores - log_total[:, :, None], MASKED_SCORE))
    prob_grad = jnp.einsum(
        "qhd,khd->hqk", dout_low, value_block, preferred_element_type=jnp.float32
    )
    score_grad = (attn_probs * (prob_grad - row_delta[:, :, None])).astype(jnp.bfloat16)
    query_grad = 0.125 * jnp.einsum(
        "hqk,khd->qhd", score_grad, key_block, preferred_element_type=jnp.float32
    )
    key_grad = 0.125 * jnp.einsum(
        "hqk,qhd->khd", score_grad, queries, preferred_element_type=jnp.float32
    )
    value_grad = jnp.einsum(
        "hqk,qhd->khd",
        attn_probs.astype(jnp.bfloat16),
        dout_low,
        preferred_element_type=jnp.float32,
    )
    bias_grad = jnp.einsum(
        "hqk,qkb->bh",
        score_grad,
        bucket_hot.astype(jnp.bfloat16),
        preferred_element_type=jnp.float32,
    )
    return (query_grad, key_grad, value_grad, bias_grad)


def per_device(
    hidden_in,
    out_grad,
    lengths,
    permutation,
    routes,
    bucket_table,
    w_qkv,
    w_out,
    w_in,
    w_down,
    w_router,
    gain_attn,
    gain_moe,
    rel_bias,
):
    stream = hidden_in[0].astype(jnp.float32)
    local_rows = stream.shape[0]
    model_width = stream.shape[1]
    head_count = rel_bias.shape[1]
    bucket_count = rel_bias.shape[0]
    head_dim = model_width // head_count
    experts = w_router.shape[1]
    slot_cap = 4 * local_rows // experts
    groups = lax.axis_size("ctx")
    perm_row = permutation[0]
    bounds = jnp.cumsum(lengths[0])
    own_start = lax.axis_index("ctx") * local_rows
    query_pos = lax.dynamic_slice_in_dim(perm_row, own_start, local_rows, 0)
    query_seg = segment_of(query_pos, bounds)
    is_valid = (query_seg < NSEQ).astype(jnp.float32)
    bucket_starts = jnp.sum(
        (bucket_table[:, None] < jnp.arange(bucket_count, dtype=jnp.int32)[None, :]).astype(
            jnp.int32
        ),
        axis=0,
    )
    qkv_full, out_full, in_full, down_full = (
        lax.all_gather(w_qkv, "wa", axis=0, tiled=True),
        lax.all_gather(w_out, "wa", axis=0, tiled=True),
        lax.all_gather(w_in[0], "wa", axis=0, tiled=True),
        lax.all_gather(w_down[0], "wa", axis=0, tiled=True),
    )
    normed_attn = rms_norm(stream, gain_attn)
    normed_attn_low = normed_attn.astype(jnp.bfloat16)
    qkv = jnp.dot(normed_attn_low, qkv_full, preferred_element_type=jnp.float32).astype(
        jnp.bfloat16
    )
    queries = qkv[:, :model_width].reshape(local_rows, head_count, head_dim)
    key_rows = qkv[:, model_width : 2 * model_width]
    value_rows = qkv[:, 2 * model_width :]
    initial = (
        jnp.full((head_count, local_rows), MASKED_SCORE, jnp.float32),
        jnp.zeros((head_count, local_rows), jnp.float32),
        jnp.zeros((head_count, local_rows, head_dim), jnp.float32),
    )
    row_max, totals, weighted = attend_piece(
        initial,
        (
            lax.all_gather(key_rows, "ctx", axis=0, tiled=True),
            lax.all_gather(value_rows, "ctx", axis=0, tiled=True),
        ),
        queries,
        query_pos,
        query_seg,
        perm_row,
        bounds,
        bucket_starts,
        rel_bias,
    )
    safe_totals = jnp.where(query_seg[None, :] < NSEQ, totals, 1.0)
    log_total = row_max + jnp.log(safe_totals)
    attn_heads = weighted / safe_totals[:, :, None]
    attn_mix = jnp.transpose(attn_heads, (1, 0, 2)).reshape(local_rows, model_width)
    attn_low = attn_mix.astype(jnp.bfloat16)
    attn_out = jnp.dot(attn_low, out_full, preferred_element_type=jnp.float32)
    resid = stream + attn_out
    normed_moe = rms_norm(resid, gain_moe)
    normed_moe_low = normed_moe.astype(jnp.bfloat16)
    normed_moe_wide = normed_moe_low.astype(jnp.float32)
    logits = jnp.dot(normed_moe_wide, w_router, precision=TOP_PRECISION)
    route_rows = routes[0]
    expert_ids = jnp.arange(experts, dtype=jnp.int32)
    first_hot = route_rows[:, 0:1] == expert_ids[None, :]
    second_hot = route_rows[:, 1:2] == expert_ids[None, :]
    chosen = jnp.stack(
        [
            jnp.sum(jnp.where(first_hot, logits, 0.0), axis=1),
            jnp.sum(jnp.where(second_hot, logits, 0.0), axis=1),
        ],
        axis=1,
    )
    gate_probs = jax.nn.softmax(chosen, axis=1)
    counts = jnp.cumsum((first_hot | second_hot).astype(jnp.int32), axis=0)
    first_slot = jnp.sum(jnp.where(first_hot, counts - 1, 0), axis=1)
    second_slot = jnp.sum(jnp.where(second_hot, counts - 1, 0), axis=1)
    first_lane = route_rows[:, 0] * slot_cap + first_slot
    second_lane = route_rows[:, 1] * slot_cap + second_slot
    lane_ids = jnp.arange(experts * slot_cap, dtype=jnp.int32)
    first_pick = (first_lane[:, None] == lane_ids[None, :]).astype(jnp.bfloat16)
    second_pick = (second_lane[:, None] == lane_ids[None, :]).astype(jnp.bfloat16)
    dispatch = (
        lead_dot(first_pick, normed_moe_low) + lead_dot(second_pick, normed_moe_low)
    ).astype(jnp.bfloat16)
    spread = jnp.broadcast_to(
        dispatch.reshape(experts, 1, slot_cap, model_width), (experts, 2, slot_cap, model_width)
    ).reshape(groups, slot_cap, model_width)
    received = lax.all_to_all(spread, "ctx", split_axis=0, concat_axis=0, tiled=True)
    item_count = received.shape[1]
    row_block = received.reshape(-1, model_width)
    gate_up = jnp.dot(row_block, in_full, preferred_element_type=jnp.float32)
    hidden = glu_act(gate_up).astype(jnp.bfloat16)
    partial_value = tail_dot(hidden, down_full).astype(jnp.bfloat16)
    returned = lax.all_to_all(
        partial_value.reshape(groups, item_count, model_width),
        "ctx",
        split_axis=0,
        concat_axis=0,
        tiled=True,
    )
    returned, gate_up_kept, received_kept = (
        returned,
        gate_up.reshape(groups, item_count, -1),
        received,
    )
    halves = returned.reshape(experts, 2, slot_cap, model_width)
    first_half = halves[:, 0].reshape(-1, model_width)
    second_half = halves[:, 1].reshape(-1, model_width)
    picked_first = jnp.dot(first_pick, first_half, preferred_element_type=jnp.float32) + jnp.dot(
        first_pick, second_half, preferred_element_type=jnp.float32
    )
    picked_second = jnp.dot(second_pick, first_half, preferred_element_type=jnp.float32) + jnp.dot(
        second_pick, second_half, preferred_element_type=jnp.float32
    )
    moe_out = gate_probs[:, 0:1] * picked_first + gate_probs[:, 1:2] * picked_second
    final = resid + moe_out
    valid_col = is_valid[:, None]
    stat_terms = jnp.stack(
        [
            jnp.sum(valid_col * final * final),
            jnp.sum(valid_col * attn_out * attn_out),
            jnp.sum(valid_col * moe_out * moe_out),
        ]
    )
    valid_count = jnp.sum(is_valid)
    grad_final = out_grad[0].astype(jnp.float32)
    first_dy = (gate_probs[:, 0:1] * grad_final).astype(jnp.bfloat16)
    second_dy = (gate_probs[:, 1:2] * grad_final).astype(jnp.bfloat16)
    gate_grad = jnp.stack(
        [jnp.sum(grad_final * picked_first, axis=1), jnp.sum(grad_final * picked_second, axis=1)],
        axis=1,
    )
    _, gate_back = jax.vjp(lambda chosen_in: jax.nn.softmax(chosen_in, axis=1), chosen)
    (chosen_grad,) = gate_back(gate_grad)
    logit_grad = jnp.where(first_hot, chosen_grad[:, 0:1], 0.0) + jnp.where(
        second_hot, chosen_grad[:, 1:2], 0.0
    )
    router_grad = lead_dot(normed_moe_wide, logit_grad, TOP_PRECISION)
    norm_moe_grad = jnp.dot(logit_grad, w_router.T, precision=TOP_PRECISION)
    dy_slots = (lead_dot(first_pick, first_dy) + lead_dot(second_pick, second_dy)).astype(
        jnp.bfloat16
    )
    dy_spread = jnp.broadcast_to(
        dy_slots.reshape(experts, 1, slot_cap, model_width), (experts, 2, slot_cap, model_width)
    ).reshape(groups, slot_cap, model_width)
    received_grad = lax.all_to_all(dy_spread, "ctx", split_axis=0, concat_axis=0, tiled=True)
    rows_grad = received_grad.reshape(-1, model_width)
    rows_kept = received_kept.reshape(-1, model_width)
    gate_up_rows = gate_up_kept.reshape(rows_grad.shape[0], -1)
    hidden_rows, act_back = jax.vjp(glu_act, gate_up_rows)
    hidden_low = hidden_rows.astype(jnp.bfloat16)
    hidden_grad_rows = jnp.dot(rows_grad, down_full, preferred_element_type=jnp.float32)
    down_grad = lead_dot(rows_grad, hidden_low)
    (gate_up_grad,) = act_back(hidden_grad_rows)
    gate_up_low = gate_up_grad.astype(jnp.bfloat16)
    in_grad = lead_dot(rows_kept, gate_up_low)
    rows_back = tail_dot(gate_up_low, in_full).astype(jnp.bfloat16)
    returned_grad = lax.all_to_all(
        rows_back.reshape(groups, slot_cap, model_width),
        "ctx",
        split_axis=0,
        concat_axis=0,
        tiled=True,
    )
    grad_halves = returned_grad.reshape(experts, 2, slot_cap, model_width)
    first_back = grad_halves[:, 0].reshape(-1, model_width)
    second_back = grad_halves[:, 1].reshape(-1, model_width)
    norm_moe_grad = (
        norm_moe_grad
        + jnp.dot(first_pick, first_back, preferred_element_type=jnp.float32)
        + jnp.dot(first_pick, second_back, preferred_element_type=jnp.float32)
    )
    norm_moe_grad = (
        norm_moe_grad
        + jnp.dot(second_pick, first_back, preferred_element_type=jnp.float32)
        + jnp.dot(second_pick, second_back, preferred_element_type=jnp.float32)
    )
    _, norm_moe_back = jax.vjp(rms_norm, resid, gain_moe)
    resid_from_norm, gain_moe_grad = norm_moe_back(norm_moe_grad)
    resid_grad = grad_final + resid_from_norm
    attn_grad_low = resid_grad.astype(jnp.bfloat16)
    out_proj_grad = lead_dot(attn_low, attn_grad_low)
    mix_grad = tail_dot(attn_grad_low, out_full)
    dout_low = mix_grad.astype(jnp.bfloat16).reshape(local_rows, head_count, head_dim)
    row_delta = jnp.einsum("qhd,hqd->hq", dout_low.astype(jnp.float32), attn_heads)
    key_all, value_all = (
        lax.all_gather(key_rows, "ctx", axis=0, tiled=True),
        lax.all_gather(value_rows, "ctx", axis=0, tiled=True),
    )
    total_rows = key_all.shape[0]
    block_rows = math.gcd(total_rows, 512)
    keys_split = key_all.reshape(total_rows, head_count, head_dim)
    values_split = value_all.reshape(total_rows, head_count, head_dim)
    seg_all = segment_of(perm_row, bounds)

    def key_step(step_index, state):
        query_acc, bias_acc, pair_buffer = state
        offset = step_index * block_rows
        key_block = lax.dynamic_slice_in_dim(keys_split, offset, block_rows, 0)
        value_block = lax.dynamic_slice_in_dim(values_split, offset, block_rows, 0)
        key_pos = lax.dynamic_slice_in_dim(perm_row, offset, block_rows, 0)
        key_seg = lax.dynamic_slice_in_dim(seg_all, offset, block_rows, 0)
        query_grad, key_grad, value_grad, bias_grad = block_grads(
            queries,
            dout_low,
            log_total,
            row_delta,
            query_pos,
            query_seg,
            key_block,
            value_block,
            key_pos,
            key_seg,
            bucket_starts,
            rel_bias,
        )
        joined = jnp.concatenate(
            [
                key_grad.reshape(block_rows, model_width),
                value_grad.reshape(block_rows, model_width),
            ],
            axis=1,
        )
        pair_buffer = lax.dynamic_update_slice_in_dim(pair_buffer, joined, offset, 0)
        return (query_acc + query_grad, bias_acc + bias_grad, pair_buffer)

    start_state = (
        jnp.zeros((local_rows, head_count, head_dim), jnp.float32),
        jnp.zeros((bucket_count, head_count), jnp.float32),
        jnp.zeros((total_rows, 2 * model_width), jnp.float32),
    )
    query_acc, bias_total, pair_buffer = lax.fori_loop(
        0, total_rows // block_rows, key_step, start_state
    )
    pair_grad = lax.psum_scatter(
        pair_buffer.astype(jnp.bfloat16), "ctx", scatter_dimension=0, tiled=True
    ).astype(jnp.float32)
    query_total = query_acc.reshape(local_rows, model_width)
    key_total = pair_grad[:, :model_width]
    value_total = pair_grad[:, model_width:]
    qkv_grad_low = jnp.concatenate([query_total, key_total, value_total], axis=1).astype(
        jnp.bfloat16
    )
    qkv_weight_grad = lead_dot(normed_attn_low, qkv_grad_low)
    norm_attn_grad = tail_dot(qkv_grad_low, qkv_full)
    _, norm_attn_back = jax.vjp(rms_norm, stream, gain_attn)
    stream_from_norm, gain_attn_grad = norm_attn_back(norm_attn_grad)
    hidden_grad = (resid_grad + stream_from_norm).astype(jnp.bfloat16)
    qkv_shard, out_shard, in_shard, down_shard = (
        lax.psum_scatter(
            qkv_weight_grad.astype(jnp.bfloat16), "wa", scatter_dimension=0, tiled=True
        ).astype(jnp.float32),
        lax.psum_scatter(
            out_proj_grad.astype(jnp.bfloat16), "wa", scatter_dimension=0, tiled=True
        ).astype(jnp.float32),
        lax.psum_scatter(
            in_grad.astype(jnp.bfloat16), "wa", scatter_dimension=0, tiled=True
        ).astype(jnp.float32),
        lax.psum_scatter(
            down_grad.astype(jnp.bfloat16), "wa", scatter_dimension=0, tiled=True
        ).astype(jnp.float32),
    )
    qkv_shard, out_shard = (
        lax.psum(qkv_shard.astype(jnp.bfloat16), "ctx").astype(jnp.float32),
        lax.psum(out_shard.astype(jnp.bfloat16), "ctx").astype(jnp.float32),
    )
    stat_sums, count_sum, router_sum, gain_attn_sum, gain_moe_sum, bias_sum = lax.psum(
        (stat_terms, valid_count, router_grad, gain_attn_grad, gain_moe_grad, bias_total),
        ("ctx", "wa"),
    )
    stats = jnp.sqrt(stat_sums / (count_sum * model_width))
    return (
        final.astype(jnp.bfloat16)[None],
        hidden_grad[None],
        qkv_shard,
        out_shard,
        in_shard[None],
        down_shard[None],
        router_sum,
        gain_attn_sum,
        gain_moe_sum,
        bias_sum,
        stats,
    )


def solution(mesh):
    placed = (
        P("wa", "ctx", None),
        P("wa", "ctx", None),
        P("wa", None),
        P("wa", None),
        P("wa", "ctx", None),
        P(),
        P("wa", None),
        P("wa", None),
        P("ctx", "wa", None),
        P("ctx", "wa", None),
        P(),
        P(),
        P(),
        P(),
    )
    return jax.shard_map(
        per_device,
        mesh=mesh,
        in_specs=placed,
        out_specs=(
            P("wa", "ctx", None),
            P("wa", "ctx", None),
            P("wa", None),
            P("wa", None),
            P("ctx", "wa", None),
            P("ctx", "wa", None),
            P(),
            P(),
            P(),
            P(),
            P(),
        ),
        check_vma=False,
    )
```

profile of v0, /device:TPU:0, one launch (start us, length us, event | category | flops | bytes accessed | tf_op | source)
XLA Modules:
  0.0 1102.4 jit_solution(17965219351237932278)
XLA Ops:
  9.6 83.1 %all-gather.9.cloned.1.call-done = bf16[1024,3072]{1,0:T(8,128)(2,1)} async-done(((bf16[512,3072]{1,0:T(8,128)(2,1)}), bf16[1024,3072]{1,0:T(8,128)(2,1)}) %all-gather.9.cloned.1.call-update) | async-done | bytes 6291472 | tf_op jit(solution)/shard_map/all_gather | solution.py:186
  92.7 3.9 convolution_convert_fusion.3
  100.5 47.8 %all-gather.11.cloned.1.call-done = bf16[2048,1024]{1,0:T(8,128)(2,1)} async-done(((bf16[128,1024]{1,0:T(8,128)(2,1)}), bf16[2048,1024]{1,0:T(8,128)(2,1)}) %all-gather.11.cloned.1.call-update) | async-done | bytes 4194320 | tf_op jit(solution)/shard_map/all_gather | solution.py:207
  148.3 6.4 copy.85
  154.7 45.4 %all-gather.13.cloned.1.call-done = bf16[2048,1024]{1,0:T(8,128)(2,1)} async-done(((bf16[128,1024]{1,0:T(8,128)(2,1)}), bf16[2048,1024]{1,0:T(8,128)(2,1)}) %all-gather.13.cloned.1.call-update) | async-done | bytes 4194320 | tf_op jit(solution)/shard_map/all_gather | solution.py:208
  200.1 6.5 copy.87
  206.7 91.9 %while.36 = (s32[]{:T(128)}, f32[16,128]{1,0:T(8,128)S(1)}, f32[16,128]{1,0:T(8,128)S(1)}, f32[16,128,64]{1,2,0:T(8,128)S(1)}, s32[128]{0:T(128)S(1)}, /*index=5...) while((s32[]{:T(128)}, f32[16,128]{1,0:T(8,128)S(1)}, ...), condition=%wide.region_9.10_spmd.clone, body=%wide.region_4.9_spmd.clone.sunk | while | flops 690574976 | bytes 51530648 | solution.py:102
  208.3 4.1 fusion.211
  212.4 5.3 copy.119
  217.7 5.6 select_reduce_fusion.6
  223.3 3.1 fusion.212
  226.8 2.5 fusion.214
  230.9 4.1 fusion.211
  235.0 5.3 copy.119
  240.3 6.4 select_reduce_fusion.6
  246.8 3.4 fusion.212
  250.9 2.5 fusion.214
  255.0 4.1 fusion.211
  259.1 5.3 copy.119
  264.4 5.6 select_reduce_fusion.6
  270.1 3.1 fusion.212
  277.6 4.1 fusion.211
  281.7 5.3 copy.119
  287.0 5.6 select_reduce_fusion.6
  292.7 3.1 fusion.212
  296.1 2.5 fusion.214
  298.7 2.9 multiply_reduce_fusion.2
  304.5 4.4 all-to-all-start
  310.6 39.5 %all-to-all-done = bf16[16,64,1024]{2,1,0:T(8,128)(2,1)} async-done(((bf16[16,64,1024]{2,1,0:T(8,128)(2,1)}), bf16[16,64,1024]{2,1,0:T(8,128)(2,1)}, u32[]{:S(2)}, u32[]{:S(2)}) %all-to-all-start) | async-done | bytes 2097184 | tf_op jit(solution)/shard_map/all_to_all | solution.py:255
  351.7 11.6 %all-to-all-start.2 = ((bf16[16,64,1024]{2,1,0:T(8,128)(2,1)}), bf16[16,64,1024]{2,1,0:T(8,128)(2,1)}, u32[]{:S(2)}, u32[]{:S(2)}) async-start(bf16[16,64,1024]{2,1,0:T(8,128)(2,1)} %bitcast.233), calls=%async_computation.2 | async-start | bytes 4194304 | tf_op jit(solution)/shard_map/all_to_all | solution.py:313
  363.9 11.8 %fusion.57 = f32[1024,2816]{1,0:T(8,128)} fusion(bf16[1024,1024]{1,0:T(8,128)(2,1)} %bitcast.24, bf16[1,1024,2816]{2,1,0:T(8,128)(2,1)} %all-gather.17.cloned.1.call-done), kind=kOutput, calls=%fused_computation.77 | convolution fusion | flops 5905580032 | bytes 19398656 | tf_op jit(solution)/shard_map/dot_general | solution.py:258
  375.7 32.9 %all-gather.19.cloned.1.call-done = bf16[1,1024,1408]{2,1,0:T(8,128)(2,1)} async-done(((bf16[1,512,1408]{2,1,0:T(8,128)(2,1)}), bf16[1,1024,1408]{2,1,0:T(8,128)(2,1)}) %all-gather.19.cloned.1.call-update) | async-done | bytes 2883600 | tf_op jit(solution)/shard_map/all_gather | solution.py:189
  408.7 14.4 %fusion.63 = (f32[1024,1408]{1,0:T(8,128)}, f32[1024,1408]{1,0:T(8,128)}, bf16[1024,1408]{1,0:T(8,128)(2,1)S(1)}) fusion(f32[1024,2816]{1,0:T(8,128)} %fusion.57, bf16[1024,1024]{1,0:T(8,128)(2,1)} %bitcast.41, bf16[1,1024,1408]{2,1,0:T(8,128)(2,1)} %all-gather.19.cloned.1.call-done), kind=kOutput, calls=%fused_computation.92 | convolution fusion | flops 2987393024 | bytes 30932992 | tf_op jit(solution)/shard_map/dot_general | solution.py:319
  423.0 4.6 fusion.67
  427.7 7.0 all-to-all-start.1
  434.7 12.5 %fusion.64 = bf16[1024,1024]{1,0:T(8,128)(2,1)} fusion(bf16[1,1024,2816]{2,1,0:T(8,128)(2,1)} %all-gather.17.cloned.1.call-done, f32[1024,1408]{1,0:T(8,128)} %get-tuple-element.707, f32[1024,1408]{1,0:T(8,128)} %get-tuple-element.706), kind=kOutput, calls=%fused_computation.93 | convolution fusion | flops 5912395776 | bytes 19398656 | tf_op jit(solution)/shard_map/dot_general | solution.py:44
  447.3 28.6 %all-to-all-done.1 = bf16[16,64,1024]{2,1,0:T(8,128)(2,1)} async-done(((bf16[16,64,1024]{2,1,0:T(8,128)(2,1)}), bf16[16,64,1024]{2,1,0:T(8,128)(2,1)}, u32[]{:S(2)}, u32[]{:S(2)}) %all-to-all-start.1) | async-done | bytes 2097184 | tf_op jit(solution)/shard_map/all_to_all | solution.py:261
  475.9 11.3 %all-to-all-start.3 = ((bf16[16,64,1024]{2,1,0:T(8,128)(2,1)}), bf16[16,64,1024]{2,1,0:T(8,128)(2,1)}, u32[]{:S(2)}, u32[]{:S(2)}) async-start(bf16[16,64,1024]{2,1,0:T(8,128)(2,1)} %bitcast.238), calls=%async_computation.3 | async-start | bytes 4194304 | tf_op jit(solution)/shard_map/all_to_all | solution.py:325
  491.3 37.0 %all-to-all-done.3 = bf16[16,64,1024]{2,1,0:T(8,128)(2,1)} async-done(((bf16[16,64,1024]{2,1,0:T(8,128)(2,1)}), bf16[16,64,1024]{2,1,0:T(8,128)(2,1)}, u32[]{:S(2)}, u32[]{:S(2)}) %all-to-all-start.3) | async-done | bytes 2097184 | tf_op jit(solution)/shard_map/all_to_all | solution.py:325
  535.8 4.3 broadcast_in_dim.251
  540.1 77.2 %while.37 = (s32[]{:T(128)}, f32[128,16,64]{0,2,1:T(8,128)S(1)}, f32[32,16]{0,1:T(8,128)S(1)}, bf16[2048,2048]{0,1:T(8,128)(2,1)}, bf16[2048,16,64]{0,2,1:T(8,12...) while((s32[]{:T(128)}, f32[128,16,64]{0,2,1:T(8,128)S(1)}, ...), condition=%wide.region_24.25_spmd.clone, body=%wide.region_22.24_spmd.clone.sunk | while | flops 1169753216 | bytes 76979128 | solution.py:399
  541.7 2.8 fusion.227
  544.8 3.8 fusion.229
  561.0 2.8 fusion.227
  564.1 3.8 fusion.229
  580.2 2.8 fusion.227
  583.3 3.8 fusion.229
  599.4 2.8 fusion.227
  602.6 3.8 fusion.229
  617.3 12.3 %copy.102 = bf16[2048,2048]{1,0:T(8,128)(2,1)} copy(bf16[2048,2048]{0,1:T(8,128)(2,1)} %get-tuple-element.492) | data formatting | bytes 16777216
  629.9 7.5 convolution_convert_fusion.2
  639.7 101.3 %reduce-scatter.16.cloned.1.call-done = bf16[128,2048]{1,0:T(8,128)(2,1)} async-done(((bf16[2048,2048]{1,0:T(8,128)(2,1)}), bf16[128,2048]{1,0:T(8,128)(2,1)}) %reduce-scatter.16.cloned.1.call-update) | async-done | bytes 524304
  742.3 4.6 convolution_convert_fusion
  747.0 13.6 %convolution_convert_fusion.1 = bf16[1024,2816]{1,0:T(8,128)(2,1)} fusion(bf16[1024,1024]{1,0:T(8,128)(2,1)} %bitcast.24, f32[1024,1408]{1,0:T(8,128)} %get-tuple-element.707, f32[1024,1408]{1,0:T(8,128)} %get-tuple-element.706), kind=kOutput, calls=%fused_computation.81 | convolution fusion | flops 5914230784 | bytes 19398656 | tf_op jit(solution)/shard_map/dot_general | solution.py:34
  763.5 20.0 %reduce-scatter.14.cloned.1.call-done = bf16[512,1408]{1,0:T(8,128)(2,1)} async-done(((bf16[1024,1408]{1,0:T(8,128)(2,1)}), bf16[512,1408]{1,0:T(8,128)(2,1)}) %reduce-scatter.14.cloned.1.call-update) | async-done | bytes 1441808 | tf_op jit(solution)/shard_map/reduce_scatter | solution.py:426
  783.5 3.1 bitcast_convert_fusion.1
  786.6 31.6 %reduce-scatter.10.cloned.1.call-done = bf16[512,1024]{1,0:T(8,128)(2,1)} async-done(((bf16[1024,1024]{1,0:T(8,128)(2,1)}), bf16[512,1024]{1,0:T(8,128)(2,1)}) %reduce-scatter.10.cloned.1.call-update) | async-done | bytes 1048592 | tf_op jit(solution)/shard_map/reduce_scatter | solution.py:420
  818.2 79.8 %reduce-scatter.8.cloned.1.call-done = bf16[512,3072]{1,0:T(8,128)(2,1)} async-done(((bf16[1024,3072]{1,0:T(8,128)(2,1)}), bf16[512,3072]{1,0:T(8,128)(2,1)}) %reduce-scatter.8.cloned.1.call-update) | async-done | bytes 3145744 | tf_op jit(solution)/shard_map/reduce_scatter | solution.py:417
  898.1 73.8 %reduce-scatter.12.cloned.1.call-done = bf16[512,2816]{1,0:T(8,128)(2,1)} async-done(((bf16[1024,2816]{1,0:T(8,128)(2,1)}), bf16[512,2816]{1,0:T(8,128)(2,1)}) %reduce-scatter.12.cloned.1.call-update) | async-done | bytes 2883600 | tf_op jit(solution)/shard_map/reduce_scatter | solution.py:423
  971.9 4.8 bitcast_convert_fusion
  976.6 5.1 fusion.73
  981.7 41.9 %all-reduce.2 = (f32[1024,8]{0,1:T(8,128)}, f32[1024]{0:T(1024)}, f32[1024]{0:T(1024)}, f32[32,16]{0,1:T(8,128)}, f32[3]{0:T(128)S(1)}, /*index=5*/f32[]{:T(128)}) all-reduce(f32[1024,8]{0,1:T(8,128)S(1)} %fusion.115, f32[1024]{0:T(1024)S(1)} %get-tuple-element.618, ...), channel_id=1, replica_groups=mesh['ctx'=16,'wa'=2] {'ctx','wa'}, use_global_device_ids=true, to_apply=%region_33.34 | all-reduce | flops 10756 | bytes 86048 | tf_op jit(solution)/shard_map/psum | solution.py:434
  1025.7 62.5 %all-reduce.6.cloned.1.call-done = (bf16[512,3072]{1,0:T(8,128)(2,1)}, bf16[512,1024]{1,0:T(8,128)(2,1)}) async-done(((bf16[512,3072]{1,0:T(8,128)(2,1)}, bf16[512,1024]{1,0:T(8,128)(2,1)}), (bf16[512,3072]{1,0:T(8,128)(2,1)}, bf16[512,1024]{1,0:T(8,128)(2,1)})) %all-reduce.6.cloned.1.call-update) | async-done | bytes 4194320 | tf_op jit(solution)/shard_map/psum | solution.py:431
  1088.1 5.5 convert_element_type.206
  (280 shorter events, 94.3 us)
Async XLA Ops:
  7.2 301.8 %copy-start = (f32[1024,8]{0,1:T(8,128)S(1)}, f32[1024,8]{0,1:T(8,128)}, u32[]{:S(2)}) copy-start(f32[1024,8]{0,1:T(8,128)} %param.28) | copy-start | bytes 98308
  7.2 85.5 %all-gather.9.cloned.1.call-start = ((), (), s32[]{:S(2)}) async-start(), calls=%async_computation.9 | async-start | bytes 9437184 | tf_op jit(solution)/shard_map/all_gather | solution.py:186
  7.9 140.4 %all-gather.11.cloned.1.call-start = ((), (), s32[]{:S(2)}) async-start(), calls=%async_computation.10 | async-start | bytes 4456448 | tf_op jit(solution)/shard_map/all_gather | solution.py:207
  9.1 0.5 copy-start.26
  9.6 83.1 %copy-start.22 = (f32[128]{0:T(128)}, f32[128]{0:T(128)S(1)}, u32[]{:S(2)}) copy-start(f32[128]{0:T(128)S(1)} %fusion.132) | copy-start | bytes 1540
  96.6 2.9 copy-start.29
  96.7 3.0 copy-start.25
  96.7 3.1 copy-start.20
  96.7 3.2 copy-start.24
  97.6 102.6 %all-gather.13.cloned.1.call-start = ((), (), s32[]{:S(2)}) async-start(), calls=%async_computation.11 | async-start | bytes 4456448 | tf_op jit(solution)/shard_map/all_gather | solution.py:208
  98.3 200.4 %all-gather.15.cloned.1.call-start = ((), (), s32[]{:S(2)}) async-start(), calls=%async_computation.12 | async-start | bytes 3145728 | tf_op jit(solution)/shard_map/all_gather | solution.py:187
  98.9 265.0 %all-gather.17.cloned.1.call-start = ((), (), s32[]{:S(2)}) async-start(), calls=%async_computation.17 | async-start | bytes 8650752 | tf_op jit(solution)/shard_map/all_gather | solution.py:188
  154.7 52.0 %copy-start.18 = (f32[32,16]{0,1:T(8,128)S(1)}, f32[32,16]{0,1:T(8,128)}, u32[]{:S(2)}) copy-start(f32[32,16]{0,1:T(8,128)} %param.31) | copy-start | bytes 6148
  206.7 92.1 %copy-start.5 = (bf16[1,128,1024]{2,1,0:T(8,128)(2,1)S(1)}, bf16[1,128,1024]{2,1,0:T(8,128)(2,1)}, u32[]{:S(2)}) copy-start(bf16[1,128,1024]{2,1,0:T(8,128)(2,1)} %param.18) | copy-start | bytes 786436
  223.3 3.4 copy-start.2
  246.7 4.2 copy-start.2
  270.1 3.4 copy-start.2
  292.7 3.4 copy-start.2
  298.6 3.1 copy-start.21
  298.7 3.7 copy-start.13
  301.8 7.2 copy-start.10
  302.9 6.5 copy-start.12
  304.5 45.5 %all-to-all-start = ((bf16[16,64,1024]{2,1,0:T(8,128)(2,1)}), bf16[16,64,1024]{2,1,0:T(8,128)(2,1)}, u32[]{:S(2)}, u32[]{:S(2)}) async-start(bf16[16,64,1024]{2,1,0:T(8,128)(2,1)} %bitcast.232), calls=%async_computation | async-start | bytes 4194304 | tf_op jit(solution)/shard_map/all_to_all | solution.py:255
  351.7 57.0 %all-to-all-start.2 = ((bf16[16,64,1024]{2,1,0:T(8,128)(2,1)}), bf16[16,64,1024]{2,1,0:T(8,128)(2,1)}, u32[]{:S(2)}, u32[]{:S(2)}) async-start(bf16[16,64,1024]{2,1,0:T(8,128)(2,1)} %bitcast.233), calls=%async_computation.2 | async-start | bytes 4194304 | tf_op jit(solution)/shard_map/all_to_all | solution.py:313
  363.3 45.4 %all-gather.19.cloned.1.call-start = ((), (), s32[]{:S(2)}) async-start(), calls=%async_computation.18 | async-start | bytes 4325376 | tf_op jit(solution)/shard_map/all_gather | solution.py:189
  408.7 14.4 %copy-start.28 = (bf16[1,1024,1408]{2,1,0:T(8,128)(2,1)S(1)}, bf16[1,1024,1408]{2,1,0:T(8,128)(2,1)}, u32[]{:S(2)}) copy-start(bf16[1,1024,1408]{2,1,0:T(8,128)(2,1)} %all-gather.19.cloned.1.call-done) | copy-start | bytes 8650756
  423.0 4.7 copy-start.30
  427.7 48.2 %all-to-all-start.1 = ((bf16[16,64,1024]{2,1,0:T(8,128)(2,1)}), bf16[16,64,1024]{2,1,0:T(8,128)(2,1)}, u32[]{:S(2)}, u32[]{:S(2)}) async-start(bf16[16,64,1024]{2,1,0:T(8,128)(2,1)} %bitcast.239), calls=%async_computation.1 | async-start | bytes 4194304 | tf_op jit(solution)/shard_map/all_to_all | solution.py:261
  475.9 52.4 %all-to-all-start.3 = ((bf16[16,64,1024]{2,1,0:T(8,128)(2,1)}), bf16[16,64,1024]{2,1,0:T(8,128)(2,1)}, u32[]{:S(2)}, u32[]{:S(2)}) async-start(bf16[16,64,1024]{2,1,0:T(8,128)(2,1)} %bitcast.238), calls=%async_computation.3 | async-start | bytes 4194304 | tf_op jit(solution)/shard_map/all_to_all | solution.py:325
  487.2 253.8 %reduce-scatter.16.cloned.1.call-start = ((), (), s32[]{:S(2)}) async-start(), calls=%async_computation.19 | async-start | bytes 8912896
  530.0 1.7 copy-start.15
  530.0 1.7 copy-start.16
  531.7 2.9 copy-start.7
  533.9 0.8 copy-start.8
  548.7 1.9 copy-start.3
  552.8 3.4 copy-start.4
  567.9 1.9 copy-start.3
  572.1 3.4 copy-start.4
  587.2 1.9 copy-start.3
  591.4 3.4 copy-start.4
  606.4 1.9 copy-start.3
  610.6 3.4 copy-start.4
  629.7 7.9 copy-start.9
  629.7 7.9 copy-start.14
  629.7 153.8 %reduce-scatter.14.cloned.1.call-start = ((), (), s32[]{:S(2)}) async-start(), calls=%async_computation.16 | async-start | bytes 4325376 | tf_op jit(solution)/shard_map/reduce_scatter | solution.py:426
  637.5 104.8 %copy-start.6 = (bf16[1,128,1024]{2,1,0:T(8,128)(2,1)S(1)}, bf16[1,128,1024]{2,1,0:T(8,128)(2,1)}, u32[]{:S(2)}) copy-start(bf16[1,128,1024]{2,1,0:T(8,128)(2,1)} %param.18) | copy-start | bytes 786436
  637.5 104.8 %copy-start.19 = (f32[1024]{0:T(1024)S(1)}, f32[1024]{0:T(1024)}, u32[]{:S(2)}) copy-start(f32[1024]{0:T(1024)} %param.29) | copy-start | bytes 12292
  637.5 104.8 %copy-start.23 = (f32[128]{0:T(128)S(1)}, f32[128]{0:T(128)}, u32[]{:S(2)}) copy-start(f32[128]{0:T(128)} %copy-done.22) | copy-start | bytes 1540
  637.5 180.7 %reduce-scatter.10.cloned.1.call-start = ((), (), s32[]{:S(2)}) async-start(), calls=%async_computation.14 | async-start | bytes 3145728 | tf_op jit(solution)/shard_map/reduce_scatter | solution.py:420
  639.6 258.4 %reduce-scatter.8.cloned.1.call-start = ((), (), s32[]{:S(2)}) async-start(), calls=%async_computation.13 | async-start | bytes 9437184 | tf_op jit(solution)/shard_map/reduce_scatter | solution.py:417
  747.0 224.9 %reduce-scatter.12.cloned.1.call-start = ((), (), s32[]{:S(2)}) async-start(), calls=%async_computation.15 | async-start | bytes 8650752 | tf_op jit(solution)/shard_map/reduce_scatter | solution.py:423
  760.6 2.7 copy-start.11
  760.6 327.5 %all-reduce.6.cloned.1.call-start = ((), (), s32[]{:S(2)}) async-start(), calls=%async_computation.20 | async-start | bytes 8388608 | tf_op jit(solution)/shard_map/psum | solution.py:431
  976.6 48.1 %copy-start.27 = (f32[128]{0:T(128)S(1)}, f32[128]{0:T(128)}, u32[]{:S(2)}) copy-start(f32[128]{0:T(128)} %copy-done.26) | copy-start | bytes 1540
  1088.1 7.1 copy-start.1
  1088.1 5.5 copy-start.17
Sparse Core Ops, SparseCore 0:
  9.6 83.0 all-gather.8
  97.7 50.5 all-gather.10
  151.0 49.0 all-gather.12
  201.5 31.6 all-gather.14
  234.6 74.4 all-gather.16
  365.3 43.2 all-gather.18
  629.8 111.1 reduce-scatter.15
  743.2 40.2 reduce-scatter.13
  786.4 31.8 reduce-scatter.9
  821.0 77.0 reduce-scatter.7
  900.5 71.3 reduce-scatter.11
  975.5 112.5 all-reduce.5
where the time goes:
time: 1110 us; the launch traced here: 1100 us
  waiting for transfers between devices  686 us (62%)
  matrix products  197 us (18%)
  local copies, waits for them, and re-layouts  74.2 us (7%)
  other arithmetic  50.9 us (5%)
  blocking collectives  41.9 us (4%)
  starting transfers between devices  35 us (3%)
  between operations  15.8 us (1%)
    unnamed x13, waiting for transfers between devices  104 us
    all_gather x1, waiting for transfers between devices, per_device(): lax.all_gather(w_qkv, 'wa', axis=0, tiled=True)  83.1 us
    reduce_scatter x1, waiting for transfers between devices, per_device(): lax.psum_scatter(qkv_weight_grad.astype(jnp.bfloat16), 'wa', scatter_dime...  79.8 us
    reduce_scatter x1, waiting for transfers between devices, per_device(): lax.psum_scatter(in_grad.astype(jnp.bfloat16), 'wa', scatter_dimension=0,...  73.8 us
    psum x1, waiting for transfers between devices, per_device(): lax.psum(qkv_shard.astype(jnp.bfloat16), 'ctx').astype(jnp.float32)  62.5 us
    all_gather x1, waiting for transfers between devices, per_device(): lax.all_gather(key_rows, 'ctx', axis=0, tiled=True)  47.8 us
    all_gather x1, waiting for transfers between devices, per_device(): lax.all_gather(value_rows, 'ctx', axis=0, tiled=True)  45.4 us
    psum x1, blocking collectives, per_device(): lax.psum((stat_terms, valid_count, router_grad, gain_attn_grad, gain_moe_...  41.9 us
  transfers between devices with their start and end apart: 16, of which 13 were waited for; matrix products, arithmetic and copies ran while one was open for 17% of the time, Pallas kernels for 0%

commit v1 on v0

--- a/solution.py
+++ b/solution.py
@@ -3,7 +3,11 @@
 import jax
 import jax.numpy as jnp
 from jax import lax
+from jax.experimental import pallas as pl
+from jax.experimental.pallas import tpu as pltpu
 from jax.sharding import PartitionSpec as P
+import functools
+import numpy as np
 
 NSEQ = 8
 
@@ -145,7 +149,7 @@
     return (query_grad, key_grad, value_grad, bias_grad)
 
 
-def per_device(
+def general_device(
     hidden_in,
     out_grad,
     lengths,
@@ -451,7 +455,684 @@
     )
 
 
+BLOCK = 256
+
+
+def nt_dot(left, right):
+    return lax.dot_general(
+        left, right, (((1,), (1,)), ((), ())), preferred_element_type=jnp.float32
+    )
+
+
+def plain_dot(left, right):
+    return jnp.dot(left, right, preferred_element_type=jnp.float32)
+
+
+def block_at(index):
+    return pl.ds(pl.multiple_of(index * BLOCK, BLOCK), BLOCK)
+
+
+def segment_begin(positions, bounds):
+    begin = positions * 0
+    for index in range(NSEQ):
+        begin = jnp.where(positions >= bounds[index], bounds[index], begin)
+    return begin
+
+
+def fill_bias_tiles(distance_rows, tiles):
+    for level in range(tiles.shape[0]):
+        spread = jnp.broadcast_to(distance_rows[level : level + 1, :], (BLOCK, 2 * BLOCK))
+        tiles[level] = pltpu.roll(spread, BLOCK + 1, 1, stride=1, stride_axis=0)[:, :BLOCK]
+
+
+def fill_sorter(perm, sorter):
+    slots = perm.shape[1]
+
+    def step(index, carry):
+        wanted = lax.broadcasted_iota(jnp.int32, (BLOCK, slots), 0) + index * BLOCK
+        sorter[block_at(index), :] = jnp.where(perm[...] == wanted, 1.0, 0.0).astype(jnp.bfloat16)
+        return carry
+
+    lax.fori_loop(0, slots // BLOCK, step, 0)
+
+
+def pair_mask(key_block, query_pos, query_begin):
+    key_pos = lax.broadcasted_iota(jnp.int32, (BLOCK, BLOCK), 0) + key_block * BLOCK
+    return (key_pos <= query_pos) & (key_pos >= query_begin)
+
+
+def attention_forward_kernel(
+    piece_count, head_dim, source, bounds, weight, perm, distance_rows, *refs
+):
+    pieces = refs[:piece_count]
+    mixed, sorted_out, rows_out, wide_out, log_out = refs[piece_count : piece_count + 5]
+    raw, sorter, tiles, mixed_sorted = refs[piece_count + 5 :]
+    slots = perm.shape[1]
+    blocks = slots // BLOCK
+    local_rows = pieces[0].shape[0]
+    for index in range(piece_count):
+        offset = pl.multiple_of(source[index] * local_rows, local_rows)
+        raw[:, pl.ds(offset, local_rows)] = nt_dot(weight[...], pieces[index][...]).astype(
+            jnp.bfloat16
+        )
+    fill_bias_tiles(distance_rows, tiles)
+    fill_sorter(perm, sorter)
+
+    def sort_step(index, carry):
+        columns = nt_dot(raw[...], sorter[block_at(index), :])
+        sorted_out[:, block_at(index)] = columns.astype(jnp.bfloat16)
+        rows_out[block_at(index), :] = jnp.transpose(columns[head_dim:]).astype(jnp.bfloat16)
+        return carry
+
+    lax.fori_loop(0, blocks, sort_step, 0)
+    mixed_sorted[...] = jnp.zeros_like(mixed_sorted)
+    total = bounds[NSEQ - 1]
+
+    def query_step(query_block, carry):
+        queries = sorted_out[:head_dim, block_at(query_block)] * 0.125
+        query_pos = lax.broadcasted_iota(jnp.int32, (1, BLOCK), 1) + query_block * BLOCK
+        query_begin = segment_begin(query_pos, bounds)
+        first = segment_begin(query_block * BLOCK, bounds) // BLOCK
+
+        def key_step(key_block, state):
+            row_max, totals, weighted = state
+            scores = plain_dot(rows_out[block_at(key_block), :head_dim], queries)
+            scores = jnp.where(
+                pair_mask(key_block, query_pos, query_begin),
+                scores + tiles[query_block - key_block],
+                MASKED_SCORE,
+            )
+            new_max = jnp.maximum(row_max, jnp.max(scores, axis=0, keepdims=True))
+            factor = jnp.exp(row_max - new_max)
+            exp_scores = jnp.exp(scores - new_max)
+            totals = totals * factor + jnp.sum(exp_scores, axis=0, keepdims=True)
+            values = sorted_out[2 * head_dim :, block_at(key_block)]
+            weighted = weighted * factor + plain_dot(values, exp_scores.astype(jnp.bfloat16))
+            return (new_max, totals, weighted)
+
+        row_max, totals, weighted = lax.fori_loop(
+            first,
+            query_block + 1,
+            key_step,
+            (
+                jnp.full((1, BLOCK), MASKED_SCORE, jnp.float32),
+                jnp.zeros((1, BLOCK), jnp.float32),
+                jnp.zeros((head_dim, BLOCK), jnp.float32),
+            ),
+        )
+        outcome = jnp.where(query_pos < total, weighted / totals, 0.0)
+        wide_out[:, block_at(query_block)] = outcome
+        log_out[:, block_at(query_block)] = row_max + jnp.log(totals)
+        mixed_sorted[:, block_at(query_block)] = outcome.astype(jnp.bfloat16)
+        return carry
+
+    lax.fori_loop(0, (total + BLOCK - 1) // BLOCK, query_step, 0)
+    for index in range(blocks):
+        columns = plain_dot(mixed_sorted[...], sorter[:, index * BLOCK : (index + 1) * BLOCK])
+        columns = columns.astype(jnp.bfloat16)
+        for part in range(BLOCK // local_rows):
+            mixed[index * (BLOCK // local_rows) + part] = columns[
+                :, part * local_rows : (part + 1) * local_rows
+            ]
+
+
+def attention_backward_kernel(
+    head_dim,
+    bounds,
+    received,
+    perm,
+    distance_rows,
+    sorted_in,
+    rows_in,
+    wide_in,
+    log_in,
+    sent,
+    grad_out,
+    distance_out,
+    dout_raw,
+    dout_sorted,
+    delta,
+    sorter,
+    tiles,
+    tile_grads,
+    grad_acc,
+    grad_sorted,
+):
+    slots = perm.shape[1]
+    blocks = slots // BLOCK
+    groups, _, local_rows = received.shape
+    for index in range(groups):
+        dout_raw[:, index * local_rows : (index + 1) * local_rows] = received[index]
+    fill_bias_tiles(distance_rows, tiles)
+    fill_sorter(perm, sorter)
+
+    def sort_step(index, carry):
+        columns = nt_dot(dout_raw[...], sorter[block_at(index), :])
+        dout_sorted[:, block_at(index)] = columns.astype(jnp.bfloat16)
+        return carry
+
+    lax.fori_loop(0, blocks, sort_step, 0)
+    tile_grads[...] = jnp.zeros_like(tile_grads)
+    grad_acc[...] = jnp.zeros_like(grad_acc)
+    total = bounds[NSEQ - 1]
+
+    def query_step(query_block, carry):
+        queries = sorted_in[:head_dim, block_at(query_block)] * 0.125
+        douts = dout_sorted[:, block_at(query_block)]
+        row_delta = jnp.sum(
+            douts.astype(jnp.float32) * wide_in[:, block_at(query_block)], axis=0, keepdims=True
+        )
+        log_total = log_in[:, block_at(query_block)]
+        query_pos = lax.broadcasted_iota(jnp.int32, (1, BLOCK), 1) + query_block * BLOCK
+        query_begin = segment_begin(query_pos, bounds)
+        inside = query_pos < total
+        first = segment_begin(query_block * BLOCK, bounds) // BLOCK
+
+        def key_step(key_block, query_grad):
+            rows = rows_in[block_at(key_block), :]
+            scores = plain_dot(rows[:, :head_dim], queries) + tiles[query_block - key_block]
+            probs = jnp.exp(
+                jnp.where(
+                    pair_mask(key_block, query_pos, query_begin) & inside,
+                    scores - log_total,
+                    MASKED_SCORE,
+                )
+            )
+            prob_grad = plain_dot(rows[:, head_dim:], douts)
+            score_grad = (probs * (prob_grad - row_delta)).astype(jnp.bfloat16)
+            tile_grads[query_block - key_block] += score_grad.astype(jnp.float32)
+            grad_acc[head_dim : 2 * head_dim, block_at(key_block)] += nt_dot(queries, score_grad)
+            grad_acc[2 * head_dim :, block_at(key_block)] += nt_dot(
+                douts, probs.astype(jnp.bfloat16)
+            )
+            keys = sorted_in[head_dim : 2 * head_dim, block_at(key_block)]
+            return query_grad + plain_dot(keys, score_grad)
+
+        query_grad = lax.fori_loop(
+            first, query_block + 1, key_step, jnp.zeros((head_dim, BLOCK), jnp.float32)
+        )
+        grad_acc[:head_dim, block_at(query_block)] = query_grad * 0.125
+        return carry
+
+    lax.fori_loop(0, (total + BLOCK - 1) // BLOCK, query_step, 0)
+    grad_sorted[...] = grad_acc[...].astype(jnp.bfloat16)
+    for index in range(blocks):
+        columns = plain_dot(grad_sorted[...], sorter[:, index * BLOCK : (index + 1) * BLOCK])
+        columns = columns.astype(jnp.bfloat16)
+        grad_out[:, index * BLOCK : (index + 1) * BLOCK] = columns
+        for part in range(BLOCK // local_rows):
+            sent[index * (BLOCK // local_rows) + part] = columns[
+                :, part * local_rows : (part + 1) * local_rows
+            ]
+    row_ids = lax.broadcasted_iota(jnp.int32, (BLOCK, BLOCK), 0)
+    column_ids = lax.broadcasted_iota(jnp.int32, (BLOCK, BLOCK), 1)
+    mirror = jnp.where(row_ids + column_ids == BLOCK - 1, 1.0, 0.0)
+    for level in range(tiles.shape[0]):
+        turned = jnp.dot(
+            mirror, tile_grads[level], precision=TOP_PRECISION, preferred_element_type=jnp.float32
+        )
+        wide = jnp.concatenate([turned, jnp.zeros((BLOCK, BLOCK), jnp.float32)], axis=1)
+        turned = pltpu.roll(wide, 0, 1, stride=1, stride_axis=0)
+        distance_out[level : level + 1, :] = jnp.sum(turned, axis=0, keepdims=True)
+
+
+def weight_gradient_kernel(piece_count, source, grads, *refs):
+    pieces = refs[:piece_count]
+    out = refs[piece_count]
+    local_rows = pieces[0].shape[0]
+    total = jnp.zeros(out.shape, jnp.float32)
+    for index in range(piece_count):
+        offset = pl.multiple_of(source[index] * local_rows, local_rows)
+        total = total + plain_dot(grads[:, pl.ds(offset, local_rows)], pieces[index][...])
+    out[...] = total
+
+
+def vmem():
+    return pl.BlockSpec(memory_space=pltpu.VMEM)
+
+
+def smem():
+    return pl.BlockSpec(memory_space=pltpu.SMEM)
+
+
+def shaped(shape, dtype):
+    return jax.ShapeDtypeStruct(shape, dtype)
+
+
+def attention_forward(source, bounds, weight, perm, distance_rows, pieces, head_dim):
+    groups = len(pieces)
+    slots = perm.shape[1]
+    local_rows = pieces[0].shape[0]
+    levels = distance_rows.shape[0]
+    flops = 2 * slots * (3 * head_dim * pieces[0].shape[1] + 4 * head_dim * slots + head_dim * slots)
+    return pl.pallas_call(
+        functools.partial(attention_forward_kernel, groups, head_dim),
+        out_shape=(
+            shaped((groups, head_dim, local_rows), jnp.bfloat16),
+            shaped((3 * head_dim, slots), jnp.bfloat16),
+            shaped((slots, 2 * head_dim), jnp.bfloat16),
+            shaped((head_dim, slots), jnp.float32),
+            shaped((1, slots), jnp.float32),
+        ),
+        in_specs=[smem(), smem()] + [vmem()] * (3 + groups),
+        out_specs=(vmem(),) * 5,
+        scratch_shapes=[
+            pltpu.VMEM((3 * head_dim, slots), jnp.bfloat16),
+            pltpu.VMEM((slots, slots), jnp.bfloat16),
+            pltpu.VMEM((levels, BLOCK, BLOCK), jnp.float32),
+            pltpu.VMEM((head_dim, slots), jnp.bfloat16),
+        ],
+        compiler_params=pltpu.CompilerParams(vmem_limit_bytes=48 << 20),
+        cost_estimate=pl.CostEstimate(
+            flops=flops, bytes_accessed=8 << 20, transcendentals=slots * slots // 4
+        ),
+    )(source, bounds, weight, perm, distance_rows, *pieces)
+
+
+def attention_backward(bounds, received, perm, distance_rows, saved, head_dim):
+    slots = perm.shape[1]
+    groups, _, local_rows = received.shape
+    levels = distance_rows.shape[0]
+    return pl.pallas_call(
+        functools.partial(attention_backward_kernel, head_dim),
+        out_shape=(
+            shaped((groups, 3 * head_dim, local_rows), jnp.bfloat16),
+            shaped((3 * head_dim, slots), jnp.bfloat16),
+            shaped((levels, 2 * BLOCK), jnp.float32),
+        ),
+        in_specs=[smem()] + [vmem()] * 7,
+        out_specs=(vmem(),) * 3,
+        scratch_shapes=[
+            pltpu.VMEM((head_dim, slots), jnp.bfloat16),
+            pltpu.VMEM((head_dim, slots), jnp.bfloat16),
+            pltpu.VMEM((1, slots), jnp.float32),
+            pltpu.VMEM((slots, slots), jnp.bfloat16),
+            pltpu.VMEM((levels, BLOCK, BLOCK), jnp.float32),
+            pltpu.VMEM((levels, BLOCK, BLOCK), jnp.float32),
+            pltpu.VMEM((3 * head_dim, slots), jnp.float32),
+            pltpu.VMEM((3 * head_dim, slots), jnp.bfloat16),
+        ],
+        compiler_params=pltpu.CompilerParams(vmem_limit_bytes=48 << 20),
+        cost_estimate=pl.CostEstimate(
+            flops=2 * slots * slots * 6 * head_dim,
+            bytes_accessed=4 << 20,
+            transcendentals=slots * slots // 4,
+        ),
+    )(bounds, received, perm, distance_rows, *saved)
+
+
+def weight_gradient(source, grads, pieces):
+    width = pieces[0].shape[1]
+    return pl.pallas_call(
+        functools.partial(weight_gradient_kernel, len(pieces)),
+        out_shape=shaped((grads.shape[0], width), jnp.float32),
+        in_specs=[smem(), vmem()] + [vmem()] * len(pieces),
+        out_specs=vmem(),
+        compiler_params=pltpu.CompilerParams(vmem_limit_bytes=32 << 20),
+        cost_estimate=pl.CostEstimate(
+            flops=2 * grads.shape[0] * grads.shape[1] * width,
+            bytes_accessed=6 << 20,
+            transcendentals=0,
+        ),
+    )(source, grads, *pieces)
+
+
+class Ring:
+    def __init__(self, groups):
+        self.chips = groups // 2
+        order = list(range(0, self.chips, 2)) + list(range(1, self.chips, 2))[::-1]
+        self.order = order
+        self.forward = self.shift(1)
+        self.backward = self.shift(-1)
+        self.swap = [(index, index ^ 1) for index in range(groups)]
+        self.same_core = [[2 * chip + core for chip in range(self.chips)] for core in range(2)]
+        table = np.zeros((groups, groups), np.int32)
+        for at, chip in enumerate(order):
+            for core in range(2):
+                steps = self.offsets()
+                near = [2 * order[(at + step) % self.chips] + core for step in steps]
+                table[2 * chip + core] = near + [index ^ 1 for index in near]
+        self.table = table
+
+    def offsets(self):
+        steps = [0]
+        for step in range(1, (self.chips + 1) // 2):
+            steps += [-step, step]
+        return steps + ([self.chips // 2] if self.chips % 2 == 0 else [])
+
+    def shift(self, step):
+        return [
+            (2 * self.order[at] + core, 2 * self.order[(at + step) % self.chips] + core)
+            for at in range(self.chips)
+            for core in range(2)
+        ]
+
+    def swapped(self, piece):
+        return lax.ppermute(piece, "ctx", self.swap)
+
+    def gather(self, piece):
+        pieces = [piece]
+        ahead = behind = piece
+        for _ in range(1, (self.chips + 1) // 2):
+            ahead = lax.ppermute(ahead, "ctx", self.forward)
+            behind = lax.ppermute(behind, "ctx", self.backward)
+            pieces += [ahead, behind]
+        if self.chips % 2 == 0:
+            half = piece.shape[0] // 2
+            pieces.append(
+                jnp.concatenate(
+                    [
+                        lax.ppermute(ahead[:half], "ctx", self.forward),
+                        lax.ppermute(behind[half:], "ctx", self.backward),
+                    ],
+                    axis=0,
+                )
+            )
+        return pieces + [self.swapped(item) for item in pieces]
+
+
+def across(values):
+    return lax.ppermute(values, "wa", [(0, 1), (1, 0)])
+
+
+def all_sum(values, groups):
+    stride = 1
+    while stride < groups:
+        values = values + lax.ppermute(
+            values, "ctx", [(index, index ^ stride) for index in range(groups)]
+        )
+        stride *= 2
+    return values + across(values)
+
+
+def flat_pack(parts, rows):
+    flat = jnp.concatenate([part.reshape(-1) for part in parts])
+    return jnp.pad(flat, (0, rows * 128 - flat.shape[0])).reshape(rows, 128)
+
+
+def fast_device(
+    hidden_in,
+    out_grad,
+    lengths,
+    permutation,
+    routes,
+    bucket_table,
+    w_qkv,
+    w_out,
+    w_in,
+    w_down,
+    w_router,
+    gain_attn,
+    gain_moe,
+    rel_bias,
+):
+    stream = hidden_in[0].astype(jnp.float32)
+    local_rows, width = stream.shape
+    bucket_count, head_count = rel_bias.shape
+    head_dim = width // head_count
+    experts = w_router.shape[1]
+    slot_cap = 4 * local_rows // experts
+    groups = lax.axis_size("ctx")
+    half_width = width // 2
+    ring = Ring(groups)
+    ctx = lax.axis_index("ctx")
+    core = ctx % 2
+    on_low = lax.axis_index("wa") == 0
+    perm_row = permutation[0]
+    slots = perm_row.shape[0]
+    bounds = jnp.cumsum(lengths[0])
+    own_start = ctx * local_rows
+    query_pos = lax.dynamic_slice_in_dim(perm_row, own_start, local_rows, 0)
+    is_valid = (segment_of(query_pos, bounds) < NSEQ).astype(jnp.float32)
+    source = lax.dynamic_index_in_dim(jnp.asarray(ring.table), ctx, 0, keepdims=False)
+
+    def in_order(own, other, axis):
+        return jnp.where(
+            on_low,
+            jnp.concatenate([own, other], axis=axis),
+            jnp.concatenate([other, own], axis=axis),
+        )
+
+    def own_first(values):
+        low, high = values[:, :half_width], values[:, half_width:]
+        return jnp.where(on_low, values, jnp.concatenate([high, low], axis=1))
+
+    def other_half(weight):
+        half = weight.shape[0] // 2
+        mine = across(lax.dynamic_slice_in_dim(weight, core * half, half, 0))
+        theirs = ring.swapped(mine)
+        return jnp.where(
+            core == 0,
+            jnp.concatenate([mine, theirs], axis=0),
+            jnp.concatenate([theirs, mine], axis=0),
+        )
+
+    head_weight = jnp.concatenate(
+        [
+            lax.dynamic_slice_in_dim(w_qkv, block * width + ctx * head_dim, head_dim, 1)
+            for block in range(3)
+        ],
+        axis=1,
+    ).T
+    head_weight = in_order(head_weight, across(head_weight), 1)
+    out_own, out_other = w_out, other_half(w_out)
+    in_weight = jnp.concatenate([w_in[0], across(w_in[0])], axis=0)
+    down_weight = jnp.concatenate([w_down[0], across(w_down[0])], axis=0)
+    qkv_other = other_half(w_qkv)
+
+    head_hot = (jnp.arange(head_count, dtype=jnp.int32) == ctx).astype(jnp.float32)
+    head_bias = jnp.sum(rel_bias * head_hot[None, :], axis=1)
+    reach = bucket_table.shape[0]
+    bucket_hot = bucket_table[:, None] == jnp.arange(bucket_count, dtype=jnp.int32)[None, :]
+    by_distance = jnp.sum(jnp.where(bucket_hot, head_bias[None, :], 0.0), axis=1)
+    levels = reach // BLOCK + 1
+    padded = jnp.pad(by_distance, (BLOCK - 1, levels * BLOCK + BLOCK - reach + 1))
+    distance_rows = jnp.stack(
+        [padded[level * BLOCK : level * BLOCK + 2 * BLOCK] for level in range(levels)]
+    )
+
+    normed_attn_low = rms_norm(stream, gain_attn).astype(jnp.bfloat16)
+    pieces = ring.gather(normed_attn_low)
+    perm_lanes = perm_row[None, :]
+    mixed, *saved = attention_forward(
+        source, bounds, head_weight, perm_lanes, distance_rows, pieces, head_dim
+    )
+    mixed = lax.all_to_all(mixed, "ctx", split_axis=0, concat_axis=0, tiled=True)
+    mixed = mixed.reshape(width, local_rows)
+    mixed_low, mixed_high = mixed[:half_width], mixed[half_width:]
+    mixed_own = jnp.where(on_low, mixed_low, mixed_high)
+    mixed_other = jnp.where(on_low, mixed_high, mixed_low)
+    attn_out = lead_dot(mixed_own, out_own) + lead_dot(mixed_other, out_other)
+    resid = stream + attn_out
+    normed_moe_low = rms_norm(resid, gain_moe).astype(jnp.bfloat16)
+    normed_moe_wide = normed_moe_low.astype(jnp.float32)
+    logits = jnp.dot(normed_moe_wide, w_router, precision=TOP_PRECISION)
+    route_rows = routes[0]
+    expert_ids = jnp.arange(experts, dtype=jnp.int32)
+    first_hot = route_rows[:, 0:1] == expert_ids[None, :]
+    second_hot = route_rows[:, 1:2] == expert_ids[None, :]
+    chosen = jnp.stack(
+        [
+            jnp.sum(jnp.where(first_hot, logits, 0.0), axis=1),
+            jnp.sum(jnp.where(second_hot, logits, 0.0), axis=1),
+        ],
+        axis=1,
+    )
+    gate_probs = jax.nn.softmax(chosen, axis=1)
+    counts = jnp.cumsum((first_hot | second_hot).astype(jnp.int32), axis=0)
+    first_slot = jnp.sum(jnp.where(first_hot, counts - 1, 0), axis=1)
+    second_slot = jnp.sum(jnp.where(second_hot, counts - 1, 0), axis=1)
+    first_lane = route_rows[:, 0] * slot_cap + first_slot
+    second_lane = route_rows[:, 1] * slot_cap + second_slot
+    lane_ids = jnp.arange(experts * slot_cap, dtype=jnp.int32)
+    first_at = first_lane[:, None] == lane_ids[None, :]
+    second_at = second_lane[:, None] == lane_ids[None, :]
+    first_pick = first_at.astype(jnp.bfloat16)
+    second_pick = second_at.astype(jnp.bfloat16)
+    any_pick = (first_at | second_at).astype(jnp.bfloat16)
+
+    def exchange(values):
+        return lax.all_to_all(
+            values,
+            "ctx",
+            split_axis=0,
+            concat_axis=0,
+            tiled=True,
+            axis_index_groups=ring.same_core,
+        )
+
+    def to_experts(rows):
+        mine = exchange(rows)
+        return jnp.concatenate([mine, ring.swapped(mine)], axis=0)
+
+    def from_experts(rows):
+        count = rows.shape[0] // 2
+        theirs = ring.swapped(rows[count:].astype(jnp.bfloat16))
+        return exchange((rows[:count] + theirs.astype(jnp.float32)).astype(jnp.bfloat16))
+
+    rows = to_experts(lead_dot(any_pick, own_first(normed_moe_low)).astype(jnp.bfloat16))
+    grad_final = out_grad[0].astype(jnp.float32)
+    slot_gate = jnp.sum(
+        jnp.where(first_at, gate_probs[:, 0:1], 0.0)
+        + jnp.where(second_at, gate_probs[:, 1:2], 0.0),
+        axis=0,
+    )
+    dy_slots = slot_gate[:, None] * lead_dot(any_pick, own_first(out_grad[0]))
+    rows_grad = to_experts(dy_slots.astype(jnp.bfloat16))
+
+    gate_up = jnp.dot(rows, in_weight, preferred_element_type=jnp.float32)
+    hidden_rows, act_back = jax.vjp(glu_act, gate_up)
+    hidden = hidden_rows.astype(jnp.bfloat16)
+    part = tail_dot(hidden, down_weight)
+    returned = own_first(from_experts(part))
+    picked_first = plain_dot(first_pick, returned)
+    picked_second = plain_dot(second_pick, returned)
+    moe_out = gate_probs[:, 0:1] * picked_first + gate_probs[:, 1:2] * picked_second
+    final = resid + moe_out
+
+    hidden_grad_rows = jnp.dot(rows_grad, down_weight, preferred_element_type=jnp.float32)
+    (gate_up_grad,) = act_back(hidden_grad_rows)
+    gate_up_low = gate_up_grad.astype(jnp.bfloat16)
+    rows_back = own_first(from_experts(tail_dot(gate_up_low, in_weight)))
+    in_other = across(lead_dot(rows[:, half_width:], gate_up_low).astype(jnp.bfloat16))
+    down_other = across(lead_dot(rows_grad[:, half_width:], hidden).astype(jnp.bfloat16))
+    in_shard = lead_dot(rows[:, :half_width], gate_up_low) + in_other.astype(jnp.float32)
+    down_shard = lead_dot(rows_grad[:, :half_width], hidden) + down_other.astype(jnp.float32)
+
+    valid_col = is_valid[:, None]
+    stat_terms = jnp.stack(
+        [
+            jnp.sum(valid_col * final * final),
+            jnp.sum(valid_col * attn_out * attn_out),
+            jnp.sum(valid_col * moe_out * moe_out),
+            jnp.sum(is_valid),
+        ]
+    )
+    gate_grad = jnp.stack(
+        [jnp.sum(grad_final * picked_first, axis=1), jnp.sum(grad_final * picked_second, axis=1)],
+        axis=1,
+    )
+    _, gate_back = jax.vjp(lambda chosen_in: jax.nn.softmax(chosen_in, axis=1), chosen)
+    (chosen_grad,) = gate_back(gate_grad)
+    logit_grad = jnp.where(first_hot, chosen_grad[:, 0:1], 0.0) + jnp.where(
+        second_hot, chosen_grad[:, 1:2], 0.0
+    )
+    router_grad = lead_dot(normed_moe_wide, logit_grad, TOP_PRECISION)
+    norm_moe_grad = jnp.dot(logit_grad, w_router.T, precision=TOP_PRECISION)
+    norm_moe_grad = norm_moe_grad + plain_dot(any_pick, rows_back)
+    _, norm_moe_back = jax.vjp(rms_norm, resid, gain_moe)
+    resid_from_norm, gain_moe_grad = norm_moe_back(norm_moe_grad)
+    resid_grad = grad_final + resid_from_norm
+    attn_grad_low = resid_grad.astype(jnp.bfloat16)
+
+    mix_grad = in_order(tail_dot(out_own, attn_grad_low), tail_dot(out_other, attn_grad_low), 0)
+    dout = lax.all_to_all(
+        mix_grad.astype(jnp.bfloat16).reshape(groups, head_dim, local_rows),
+        "ctx",
+        split_axis=0,
+        concat_axis=0,
+        tiled=True,
+    )
+    out_from_other = across(plain_dot(mixed_other, attn_grad_low).astype(jnp.bfloat16))
+    out_shard = plain_dot(mixed_own, attn_grad_low) + out_from_other.astype(jnp.float32)
+    out_shard = lax.psum(out_shard.astype(jnp.bfloat16), "ctx").astype(jnp.float32)
+
+    sent, head_grads, distance_grads = attention_backward(
+        bounds, dout, perm_lanes, distance_rows, saved, head_dim
+    )
+    qkv_grad = lax.all_to_all(sent, "ctx", split_axis=0, concat_axis=0, tiled=True)
+    qkv_grad = jnp.transpose(qkv_grad.reshape(head_count, 3, head_dim, local_rows), (1, 0, 2, 3))
+    qkv_grad = qkv_grad.reshape(3 * width, local_rows)
+
+    def feature_grad(weight):
+        return lax.dot_general(
+            qkv_grad, weight, (((0,), (1,)), ((), ())), preferred_element_type=jnp.float32
+        )
+
+    norm_attn_grad = in_order(feature_grad(w_qkv), feature_grad(qkv_other), 1)
+    _, norm_attn_back = jax.vjp(rms_norm, stream, gain_attn)
+    stream_from_norm, gain_attn_grad = norm_attn_back(norm_attn_grad)
+    hidden_grad = (resid_grad + stream_from_norm).astype(jnp.bfloat16)
+
+    head_total = weight_gradient(source, head_grads, pieces)
+    low_part, high_part = head_total[:, :half_width], head_total[:, half_width:]
+    head_other = across(jnp.where(on_low, high_part, low_part).astype(jnp.bfloat16))
+    head_shard = jnp.where(on_low, low_part, high_part) + head_other.astype(jnp.float32)
+    gathered = jnp.stack(ring.gather(head_shard.astype(jnp.bfloat16)))
+    back = lax.dynamic_index_in_dim(
+        jnp.asarray(np.argsort(ring.table, axis=1).astype(np.int32)), ctx, 0, keepdims=False
+    )
+    gathered = jnp.take(gathered, back, axis=0)
+    gathered = gathered.reshape(head_count, 3, head_dim, half_width)
+    qkv_shard = jnp.transpose(gathered, (3, 1, 0, 2)).reshape(half_width, 3 * width)
+    qkv_shard = qkv_shard.astype(jnp.float32)
+
+    spread_len = levels * BLOCK + BLOCK
+    by_distance_grad = sum(
+        jnp.pad(distance_grads[level], (level * BLOCK, spread_len - (level + 2) * BLOCK))
+        for level in range(levels)
+    )[BLOCK - 1 : BLOCK - 1 + reach]
+    head_bias_grad = jnp.sum(jnp.where(bucket_hot, by_distance_grad[:, None], 0.0), axis=0)
+    bias_grad = head_bias_grad[:, None] * head_hot[None, :]
+
+    early = all_sum(flat_pack((router_grad, gain_moe_grad, stat_terms), 80), groups)
+    late = all_sum(flat_pack((gain_attn_grad, bias_grad), 16), groups)
+    early, late = early.reshape(-1), late.reshape(-1)
+    router_sum = early[: width * experts].reshape(width, experts)
+    gain_moe_sum = early[width * experts : width * (experts + 1)]
+    sums = early[width * (experts + 1) : width * (experts + 1) + 4]
+    gain_attn_sum = late[:width]
+    bias_sum = late[width : width + bucket_count * head_count].reshape(bucket_count, head_count)
+    stats = jnp.sqrt(sums[:3] / (sums[3] * width))
+    return (
+        final.astype(jnp.bfloat16)[None],
+        hidden_grad[None],
+        qkv_shard,
+        out_shard,
+        in_shard[None],
+        down_shard[None],
+        router_sum,
+        gain_attn_sum,
+        gain_moe_sum,
+        bias_sum,
+        stats,
+    )
+
+
+def choose_device(groups, planes, *arguments):
+    w_router, rel_bias = arguments[10], arguments[13]
+    local_rows = arguments[0].shape[1]
+    fits = (
+        planes == 2
+        and rel_bias.shape[1] == groups
+        and 2 * w_router.shape[1] == groups
+        and local_rows == 128
+    )
+    return (fast_device if fits else general_device)(*arguments)
+
+
 def solution(mesh):
+    per_device = functools.partial(choose_device, mesh.shape["ctx"], mesh.shape["wa"])
     placed = (
         P("wa", "ctx", None),
         P("wa", "ctx", None),

time: 1110 us -> 581 us (0.52)
  waiting for transfers between devices: 686 us -> 225 us
  matrix products: 197 us -> 107 us
  starting transfers between devices: 35 us -> 86 us
  blocking collectives: 41.9 us -> 0 us
  Pallas kernels: 0 us -> 40.4 us
  other arithmetic: 50.9 us -> 30.7 us
    all_gather x6 -> x0, waiting for transfers between devices: 209 us -> none  [the longest x1 83.1 us: per_device(): lax.all_gather(w_qkv, 'wa', axis=0, tiled=True)]
    reduce_scatter x4 -> x0, waiting for transfers between devices: 205 us -> none  [the longest x1 79.8 us: per_device(): lax.psum_scatter(qkv_weight_grad.astype(jnp.bfloat16), 'wa', scatter_dime...]
    ppermute x0 -> x57, waiting for transfers between devices: none -> 148 us  [the longest x11 97.1 us: across(): return lax.ppermute(values, 'wa', [(0, 1), (1, 0)])]
    unnamed x13 -> x1, waiting for transfers between devices: 104 us -> 0.02 us
    dot_general x54 -> x11, matrix products: 144 us -> 48 us  [the longest x5 13.9 us: plain_dot(): return jnp.dot(left, right, preferred_element_type=jnp.float32)]
    psum x1, waiting for transfers between devices: 62.5 us -> 10.9 us  [fast_device(): lax.psum(out_shard.astype(jnp.bfloat16), 'ctx').astype(jnp.float32)]
    ppermute x0 -> x57, starting transfers between devices: none -> 48.7 us  [the longest x6 17.2 us: gather(): ahead = lax.ppermute(ahead, 'ctx', self.forward)]
    psum x1 -> x0, blocking collectives: 41.9 us -> none  [per_device(): lax.psum((stat_terms, valid_count, router_grad, gain_attn_grad, gain_moe_...]
  transfers between devices with their start and end apart: 16 -> 65, of which waited for: 13 -> 25; matrix products, arithmetic and copies ran while one was open for 17% -> 33% of each run, Pallas kernels for 0% -> 7%
where the time goes in v1:
time: 581 us; the launch traced here: 572 us
  waiting for transfers between devices  225 us (39%)
  matrix products  107 us (18%)
  starting transfers between devices  86 us (15%)
  local copies, waits for them, and re-layouts  67.1 us (12%)
  Pallas kernels  40.4 us (7%)
  other arithmetic  30.7 us (5%)
  between operations  16.1 us (3%)
    ppermute x11, waiting for transfers between devices, across(): return lax.ppermute(values, 'wa', [(0, 1), (1, 0)])  97.1 us
    all_to_all x4, waiting for transfers between devices, exchange(): lax.all_to_all(values, 'ctx', split_axis=0, concat_axis=0, tiled=True, ax...  57.1 us
    dot_general x9, matrix products, lead_dot(): lax.dot_general(left, right, (((0,), (0,)), ((), ())), precision=precisio...  36.6 us
    unnamed x124, local copies, waits for them, and re-layouts  33.8 us
    ppermute x6, waiting for transfers between devices, gather(): ahead = lax.ppermute(ahead, 'ctx', self.forward)  30.7 us
    dot_general x4, matrix products, tail_dot(): lax.dot_general(left, right, (((1,), (1,)), ((), ())), preferred_element_...  22.6 us
    all_to_all x4, starting transfers between devices, exchange(): lax.all_to_all(values, 'ctx', split_axis=0, concat_axis=0, tiled=True, ax...  20.8 us
    pallas_call x1, Pallas kernels, attention_forward(): pl.pallas_call(functools.partial(attention_forward_kernel, groups, head_d...  18.7 us
  transfers between devices with their start and end apart: 65, of which 25 were waited for; matrix products, arithmetic and copies ran while one was open for 33% of the time, Pallas kernels for 7%

profile of v1, /device:TPU:0, one launch (start us, length us, event | category | flops | bytes accessed | tf_op | source)
XLA Modules:
  0.0 572.0 jit_solution(14029406118546480912)
XLA Ops:
  10.5 3.1 collective-permute-start.1
  13.6 6.2 %collective-permute-done.1.refs_1_ = bf16[128,1024]{1,0:T(8,128)(2,1)S(1)} collective-permute-done((bf16[128,1024]{1,0:T(8,128)(2,1)S(1)}, bf16[128,1024]{1,0:T(8,128)(2,1)S(1)}, u32[]{:S(2)}, u32[]{:S(2)}) %collective-permute-start.1) | collective-permute-done | bytes 262176 | tf_op jit(solution)/shard_map/ppermute | solution.py:817
  19.8 1.8 collective-permute-start.3
  23.4 3.8 collective-permute-done.3.refs_3_
  31.2 2.6 collective-permute-done.5.refs_5_
  45.9 2.3 collective-permute-done
  55.2 18.7 %shard_map.239 = (bf16[16,64,128]{2,1,0:T(8,128)(2,1)S(1)}, bf16[192,2048]{1,0:T(8,128)(2,1)}, bf16[2048,128]{1,0:T(8,128)(2,1)S(1)}, f32[64,2048]{1,0:T(8,128)S(1)}, f32[1,2048]{1,0:T(1,128)S(1)}) custom-call(s32[16]{0:T(128)S(1)} %fusion.85.source, s32[8]{0:T(128)S(1)} %bitcast.179, bf16[192,1024]{1,0:T(8,128)(2,1)S(1)} %maximum_select_fusion.8.weight, ...), custom_call_target="tpu_custom_call" | custom-call | flops 3489660928 | bytes 8388608 | tf_op jit(solution)/shard_map/pallas_call | solution.py:708
  76.1 6.0 %all-to-all-start = ((bf16[16,64,128]{2,1,0:T(8,128)(2,1)}), bf16[16,64,128]{2,1,0:T(8,128)(2,1)}, u32[]{:S(2)}, u32[]{:S(2)}) async-start(bf16[16,64,128]{2,1,0:T(8,128)(2,1)} %copy-done.1), calls=%async_computation | async-start | bytes 524288 | tf_op jit(solution)/shard_map/all_to_all | solution.py:940
  84.4 7.8 %all-to-all-done = bf16[16,64,128]{2,1,0:T(8,128)(2,1)} async-done(((bf16[16,64,128]{2,1,0:T(8,128)(2,1)}), bf16[16,64,128]{2,1,0:T(8,128)(2,1)}, u32[]{:S(2)}, u32[]{:S(2)}) %all-to-all-start) | async-done | bytes 262176 | tf_op jit(solution)/shard_map/all_to_all | solution.py:940
  93.9 2.9 multiply_reduce_fusion.2
  99.2 4.2 all-to-all-start.1
  106.6 2.5 multiply_convert_fusion.1
  109.1 20.5 %all-to-all-done.1 = bf16[8,64,1024]{2,1,0:T(8,128)(2,1)} async-done(((bf16[8,64,1024]{2,1,0:T(8,128)(2,1)}), bf16[8,64,1024]{2,1,0:T(8,128)(2,1)}, u32[]{:S(2)}, u32[]{:S(2)}) %all-to-all-start.1) | async-done | bytes 1048608 | tf_op jit(solution)/shard_map/all_to_all | solution.py:975
  129.5 4.7 all-to-all-start.3
  134.9 2.7 constant_dynamic-slice_fusion.2
  139.2 20.7 %all-to-all-done.3 = bf16[8,64,1024]{2,1,0:T(8,128)(2,1)} async-done(((bf16[8,64,1024]{2,1,0:T(8,128)(2,1)}), bf16[8,64,1024]{2,1,0:T(8,128)(2,1)}, u32[]{:S(2)}, u32[]{:S(2)}) %all-to-all-start.3) | async-done | bytes 1048608 | tf_op jit(solution)/shard_map/all_to_all | solution.py:975
  160.6 8.7 %collective-permute-done.20 = bf16[512,2816]{1,0:T(8,128)(2,1)} collective-permute-done((bf16[512,2816]{1,0:T(8,128)(2,1)}, bf16[512,2816]{1,0:T(8,128)(2,1)}, u32[]{:S(2)}, u32[]{:S(2)}) %collective-permute-start.20) | collective-permute-done | bytes 2883616 | tf_op jit(solution)/shard_map/ppermute | solution.py:835
  169.2 11.8 %fusion.7 = f32[1024,2816]{1,0:T(8,128)} fusion(bf16[512,2816]{1,0:T(8,128)(2,1)} %collective-permute-done.20, bf16[512,2816]{1,0:T(8,128)(2,1)} %bitcast.224, bf16[512,1024]{1,0:T(8,128)(2,1)} %collective-permute-done.19, bf16[512,1024]{1,0:T(8,128)(2,1)} %bitcast.24), kind=kOutput, calls=%fused_computation.16 | convolution fusion | flops 5921308672 | bytes 19398656 | tf_op jit(solution)/shard_map/dot_general | solution.py:1003
  181.0 19.1 %collective-permute-done.21 = bf16[512,1408]{1,0:T(8,128)(2,1)} collective-permute-done((bf16[512,1408]{1,0:T(8,128)(2,1)}, bf16[512,1408]{1,0:T(8,128)(2,1)}, u32[]{:S(2)}, u32[]{:S(2)}) %collective-permute-start.21) | collective-permute-done | bytes 1441824 | tf_op jit(solution)/shard_map/ppermute | solution.py:835
  200.1 13.0 %fusion.20 = (f32[1024,1408]{1,0:T(8,128)S(1)}, f32[1024,1408]{1,0:T(8,128)}, bf16[1024,1408]{1,0:T(8,128)(2,1)S(1)}) fusion(f32[1024,2816]{1,0:T(8,128)} %fusion.7, bf16[512,1408]{1,0:T(8,128)(2,1)} %collective-permute-done.21, bf16[512,1408]{1,0:T(8,128)(2,1)S(1)} %bitcast.227, bf16[512,1024]{1,0:T(8,128)(2,1)S(1)} %collective-permute-done.23, ...), kind=kOutput, calls=%fused_computation.50 | convolution fusion | flops 2997354496 | bytes 30932992 | tf_op jit(solution)/shard_map/dot_general | solution.py:1013
  213.2 5.9 %fusion.21 = f32[1024,1024]{1,0:T(8,128)S(1)} fusion(bf16[1024,1408]{1,0:T(8,128)(2,1)S(1)} %get-tuple-element.71, bf16[512,1408]{1,0:T(8,128)(2,1)} %collective-permute-done.21, bf16[512,1408]{1,0:T(8,128)(2,1)S(1)} %bitcast.228), kind=kOutput, calls=%fused_computation.51 | convolution fusion | flops 2958557184 | bytes 9961472 | tf_op jit(solution)/shard_map/dot_general | solution.py:48
  219.1 2.0 copy-done.17
  221.4 7.7 %convolution_convert_fusion = bf16[512,2816]{1,0:T(8,128)(2,1)} fusion(bf16[512,1024]{1,0:T(8,128)(2,1)} %bitcast.24, bf16[512,1024]{1,0:T(8,128)(2,1)} %collective-permute-done.19, f32[1024,1408]{1,0:T(8,128)} %get-tuple-element.70, f32[1024,1408]{1,0:T(8,128)S(1)} %get-tuple-element.69), kind=kOutput, calls=%fused_computation.14 | convolution fusion | flops 2962096128 | bytes 16515072 | tf_op jit(solution)/shard_map/dot_general | solution.py:38
  229.6 14.2 %fusion.6 = f32[1024,1024]{1,0:T(8,128)} fusion(bf16[512,2816]{1,0:T(8,128)(2,1)} %collective-permute-done.20, bf16[512,2816]{1,0:T(8,128)(2,1)} %bitcast.225, f32[1024,1408]{1,0:T(8,128)} %get-tuple-element.70, f32[1024,1408]{1,0:T(8,128)} %copy-done.50), kind=kOutput, calls=%fused_computation.15 | convolution fusion | flops 5922881536 | bytes 21495808 | tf_op jit(solution)/shard_map/dot_general | solution.py:48
  243.8 2.7 slice.334
  246.7 4.2 convolution_convert_fusion.1
  256.2 6.2 %all-to-all-start.2 = ((bf16[8,64,1024]{2,1,0:T(8,128)(2,1)}), bf16[8,64,1024]{2,1,0:T(8,128)(2,1)}, u32[]{:S(2)}, u32[]{:S(2)}) async-start(bf16[8,64,1024]{2,1,0:T(8,128)(2,1)} %bitcast.186), calls=%async_computation.2 | async-start | bytes 2097152 | tf_op jit(solution)/shard_map/all_to_all | solution.py:975
  262.4 3.3 fusion.18
  265.8 59.6 %collective-permute-done.46 = bf16[512,1408]{1,0:T(8,128)(2,1)} collective-permute-done((bf16[512,1408]{1,0:T(8,128)(2,1)}, bf16[512,1408]{1,0:T(8,128)(2,1)}, u32[]{:S(2)}, u32[]{:S(2)}) %collective-permute-start.46) | collective-permute-done | bytes 1441824 | tf_op jit(solution)/shard_map/ppermute | solution.py:835
  325.4 5.0 fusion.8
  330.4 11.2 %add_bitcast_fusion = f32[1,512,2816]{2,1,0:T(8,128)} fusion(bf16[512,2816]{1,0:T(8,128)(2,1)} %collective-permute-done.45, bf16[512,1024]{1,0:T(8,128)(2,1)} %bitcast.24, bf16[512,1024]{1,0:T(8,128)(2,1)} %collective-permute-done.19, f32[1024,1408]{1,0:T(8,128)} %get-tuple-element.70, f32[1024,1408]{1,0:T(8,128)} %copy-done.50), kind=kOutput, calls=%fused_computation.11 | convolution fusion | flops 2963537920 | bytes 22282240 | tf_op jit(solution)/shard_map/dot_general | solution.py:38
  341.6 5.7 all-to-all-start.4
  350.4 2.7 fusion.37
  357.1 15.9 %all-to-all-done.4 = bf16[8,64,1024]{2,1,0:T(8,128)(2,1)} async-done(((bf16[8,64,1024]{2,1,0:T(8,128)(2,1)}), bf16[8,64,1024]{2,1,0:T(8,128)(2,1)}, u32[]{:S(2)}, u32[]{:S(2)}) %all-to-all-start.4) | async-done | bytes 1048608 | tf_op jit(solution)/shard_map/all_to_all | solution.py:975
  374.4 4.4 fusion.43
  378.7 2.6 concatenate.90
  384.9 2.1 collective-permute-done.48
  387.1 2.0 fusion.57
  389.1 1.9 collective-permute-done.49
  393.7 5.1 all-to-all-start.5
  399.1 2.4 convolution_convert_fusion.2
  405.1 1.8 copy.64
  412.2 18.5 %shard_map.240 = (bf16[16,192,128]{2,1,0:T(8,128)(2,1)}, bf16[192,2048]{1,0:T(8,128)(2,1)S(1)}, f32[5,512]{1,0:T(8,128)S(1)}) custom-call(s32[8]{0:T(128)S(1)} %bitcast.181, bf16[16,64,128]{2,1,0:T(8,128)(2,1)} %all-to-all-done.5.received, s32[1,2048]{1,0:T(1,128)S(1)} %copy-done.2, f32[5,512]{1,0:T(8,128)S(1)} %stack.104.distance_rows, ...), custom_call_target="tpu_custom_call" | custom-call | flops 3221225472 | bytes 4194304 | tf_op jit(solution)/shard_map/pallas_call | solution.py:736
  430.7 3.2 shard_map.241
  434.5 6.3 %collective-permute-done.27 = bf16[192,512]{1,0:T(8,128)(2,1)S(1)} collective-permute-done((bf16[192,512]{1,0:T(8,128)(2,1)S(1)}, bf16[192,512]{1,0:T(8,128)(2,1)S(1)}, u32[]{:S(2)}, u32[]{:S(2)}) %collective-permute-start.27) | collective-permute-done | bytes 196640 | tf_op jit(solution)/shard_map/ppermute | solution.py:835
  443.8 5.4 all-to-all-start.6
  453.2 2.6 add_convert_fusion.1
  455.8 13.2 %collective-permute-done.30 = bf16[192,512]{1,0:T(8,128)(2,1)S(1)} collective-permute-done((bf16[192,512]{1,0:T(8,128)(2,1)S(1)}, bf16[192,512]{1,0:T(8,128)(2,1)S(1)}, u32[]{:S(2)}, u32[]{:S(2)}) %collective-permute-start.30) | collective-permute-done | bytes 196640 | tf_op jit(solution)/shard_map/ppermute | solution.py:817
  471.4 7.8 %collective-permute-start.32 = (bf16[192,512]{1,0:T(8,128)(2,1)S(1)}, bf16[192,512]{1,0:T(8,128)(2,1)S(1)}, u32[]{:S(2)}, u32[]{:S(2)}) collective-permute-start(bf16[192,512]{1,0:T(8,128)(2,1)S(1)} %collective-permute-done.30), channel_id=1, source_target_pairs={{0,8},{2,10},{8,16},{10,18},{16,24},{18,26},{24,28},{26,30},{28,20... | collective-permute-start | bytes 589832 | tf_op jit(solution)/shard_map/ppermute | solution.py:817
  479.8 4.9 collective-permute-done.32
  484.7 3.3 collective-permute-start.33
  488.7 4.8 collective-permute-done.33
  494.6 3.9 collective-permute-done.34
  498.5 2.3 collective-permute-start.35
  501.4 2.0 collective-permute-done.35
  511.8 3.1 fusion.123
  514.9 3.5 fusion.9
  520.9 2.1 collective-permute-start.53
  524.6 4.3 gather_fusion
  529.8 5.0 fusion.15
  534.8 6.6 %copy.63 = f32[512,3072]{1,0:T(8,128)} copy(f32[512,3072]{0,1:T(8,128)} %bitcast.182) | data formatting | bytes 12582912
  541.4 10.9 %all-reduce.12.cloned.1.call-done = bf16[512,1024]{1,0:T(8,128)(2,1)} async-done(((bf16[512,1024]{1,0:T(8,128)(2,1)}), bf16[512,1024]{1,0:T(8,128)(2,1)}) %all-reduce.12.cloned.1.call-update) | async-done | bytes 1048592 | tf_op jit(solution)/shard_map/psum | solution.py:1058
  552.3 2.8 convert_element_type.168
  556.9 2.8 collective-permute-done.55
  (316 shorter events, 104.8 us)
Async XLA Ops:
  10.5 9.3 %collective-permute-start.1 = (bf16[128,1024]{1,0:T(8,128)(2,1)S(1)}, bf16[128,1024]{1,0:T(8,128)(2,1)S(1)}, u32[]{:S(2)}, u32[]{:S(2)}) collective-permute-start(bf16[128,1024]{1,0:T(8,128)(2,1)S(1)} %fusion.35.refs_0_), channel_id=1, source_target_pairs={{0,8},{2,10},{8,16},{10,18},{16,24},{18,26},{24,28},{26,30},{28,20... | collective-permute-start | bytes 786440 | tf_op jit(solution)/shard_map/ppermute | solution.py:817
  13.5 8.8 %collective-permute-start.2 = (bf16[128,1024]{1,0:T(8,128)(2,1)S(1)}, bf16[128,1024]{1,0:T(8,128)(2,1)S(1)}, u32[]{:S(2)}, u32[]{:S(2)}) collective-permute-start(bf16[128,1024]{1,0:T(8,128)(2,1)S(1)} %fusion.35.refs_0_), channel_id=1, source_target_pairs={{0,4},{2,6},{8,0},{10,2},{16,8},{18,10},{24,16},{26,18},{28,24},{3... | collective-permute-start | bytes 786440 | tf_op jit(solution)/shard_map/ppermute | solution.py:818
  13.5 34.7 %collective-permute-start.9 = (bf16[128,1024]{1,0:T(8,128)(2,1)S(1)}, bf16[128,1024]{1,0:T(8,128)(2,1)S(1)}, u32[]{:S(2)}, u32[]{:S(2)}) collective-permute-start(bf16[128,1024]{1,0:T(8,128)(2,1)S(1)} %fusion.35.refs_0_), channel_id=1, source_target_pairs={{0,2},{2,0},{4,6},{6,4},{8,10},{10,8},{12,14},{14,12},{16,18},{18,... | collective-permute-start | bytes 786440 | tf_op jit(solution)/shard_map/ppermute | solution.py:811
  19.8 7.5 %collective-permute-start.3 = (bf16[128,1024]{1,0:T(8,128)(2,1)S(1)}, bf16[128,1024]{1,0:T(8,128)(2,1)S(1)}, u32[]{:S(2)}, u32[]{:S(2)}) collective-permute-start(bf16[128,1024]{1,0:T(8,128)(2,1)S(1)} %collective-permute-done.1.refs_1_), channel_id=1, source_target_pairs={{0,8},{2,10},{8,16},{10,18},{16,24},{18,26},{24,28},{26,30},{28,20... | collective-permute-start | bytes 786440 | tf_op jit(solution)/shard_map/ppermute | solution.py:817
  22.4 7.0 %collective-permute-start.4 = (bf16[128,1024]{1,0:T(8,128)(2,1)S(1)}, bf16[128,1024]{1,0:T(8,128)(2,1)S(1)}, u32[]{:S(2)}, u32[]{:S(2)}) collective-permute-start(bf16[128,1024]{1,0:T(8,128)(2,1)S(1)} %collective-permute-done.2.refs_2_), channel_id=1, source_target_pairs={{0,4},{2,6},{8,0},{10,2},{16,8},{18,10},{24,16},{26,18},{28,24},{3... | collective-permute-start | bytes 786440 | tf_op jit(solution)/shard_map/ppermute | solution.py:818
  27.3 6.6 %collective-permute-start.5 = (bf16[128,1024]{1,0:T(8,128)(2,1)S(1)}, bf16[128,1024]{1,0:T(8,128)(2,1)S(1)}, u32[]{:S(2)}, u32[]{:S(2)}) collective-permute-start(bf16[128,1024]{1,0:T(8,128)(2,1)S(1)} %collective-permute-done.3.refs_3_), channel_id=1, source_target_pairs={{0,8},{2,10},{8,16},{10,18},{16,24},{18,26},{24,28},{26,30},{28,20... | collective-permute-start | bytes 786440 | tf_op jit(solution)/shard_map/ppermute | solution.py:817
  29.4 9.1 %collective-permute-start.6 = (bf16[128,1024]{1,0:T(8,128)(2,1)S(1)}, bf16[128,1024]{1,0:T(8,128)(2,1)S(1)}, u32[]{:S(2)}, u32[]{:S(2)}) collective-permute-start(bf16[128,1024]{1,0:T(8,128)(2,1)S(1)} %collective-permute-done.4.refs_4_), channel_id=1, source_target_pairs={{0,4},{2,6},{8,0},{10,2},{16,8},{18,10},{24,16},{26,18},{28,24},{3... | collective-permute-start | bytes 786440 | tf_op jit(solution)/shard_map/ppermute | solution.py:818
  34.5 7.0 %collective-permute-start.7 = (bf16[64,1024]{1,0:T(8,128)(2,1)}, bf16[64,1024]{1,0:T(8,128)(2,1)}, u32[]{:S(2)}, u32[]{:S(2)}) collective-permute-start(bf16[64,1024]{1,0:T(8,128)(2,1)} %slice.221), channel_id=1, source_target_pairs={{0,8},{2,10},{8,16},{10,18},{16,24},{18,26},{24,28},{26,30},{28,20... | collective-permute-start | bytes 393224 | tf_op jit(solution)/shard_map/ppermute | solution.py:825
  38.0 10.8 %collective-permute-start.10 = (bf16[128,1024]{1,0:T(8,128)(2,1)S(1)}, bf16[128,1024]{1,0:T(8,128)(2,1)}, u32[]{:S(2)}, u32[]{:S(2)}) collective-permute-start(bf16[128,1024]{1,0:T(8,128)(2,1)S(1)} %collective-permute-done.1.refs_1_), channel_id=1, source_target_pairs={{0,2},{2,0},{4,6},{6,4},{8,10},{10,8},{12,14},{14,12},{16,18},{18,... | collective-permute-start | bytes 786440 | tf_op jit(solution)/shard_map/ppermute | solution.py:811
  38.0 10.8 %collective-permute-start.11 = (bf16[128,1024]{1,0:T(8,128)(2,1)S(1)}, bf16[128,1024]{1,0:T(8,128)(2,1)}, u32[]{:S(2)}, u32[]{:S(2)}) collective-permute-start(bf16[128,1024]{1,0:T(8,128)(2,1)S(1)} %collective-permute-done.2.refs_2_), channel_id=1, source_target_pairs={{0,2},{2,0},{4,6},{6,4},{8,10},{10,8},{12,14},{14,12},{16,18},{18,... | collective-permute-start | bytes 786440 | tf_op jit(solution)/shard_map/ppermute | solution.py:811
  39.2 5.8 %collective-permute-start.8 = (bf16[64,1024]{1,0:T(8,128)(2,1)}, bf16[64,1024]{1,0:T(8,128)(2,1)}, u32[]{:S(2)}, u32[]{:S(2)}) collective-permute-start(bf16[64,1024]{1,0:T(8,128)(2,1)} %slice.222), channel_id=1, source_target_pairs={{0,4},{2,6},{8,0},{10,2},{16,8},{18,10},{24,16},{26,18},{28,24},{3... | collective-permute-start | bytes 393224 | tf_op jit(solution)/shard_map/ppermute | solution.py:826
  41.4 6.8 %collective-permute-start = (bf16[192,512]{1,0:T(8,128)(2,1)}, bf16[192,512]{1,0:T(8,128)(2,1)S(1)}, u32[]{:S(2)}, u32[]{:S(2)}) collective-permute-start(bf16[192,512]{1,0:T(8,128)(2,1)} %maximum_bitcast_fusion), channel_id=1, source_target_pairs={{0,1},{1,0},{2,3},{3,2},{4,5},{5,4},{6,7},{7,6},{8,9},{9,8},{10,11... | collective-permute-start | bytes 589832 | tf_op jit(solution)/shard_map/ppermute | solution.py:835
  45.0 8.8 %collective-permute-start.12 = (bf16[128,1024]{1,0:T(8,128)(2,1)S(1)}, bf16[128,1024]{1,0:T(8,128)(2,1)}, u32[]{:S(2)}, u32[]{:S(2)}) collective-permute-start(bf16[128,1024]{1,0:T(8,128)(2,1)S(1)} %collective-permute-done.3.refs_3_), channel_id=1, source_target_pairs={{0,2},{2,0},{4,6},{6,4},{8,10},{10,8},{12,14},{14,12},{16,18},{18,... | collective-permute-start | bytes 786440 | tf_op jit(solution)/shard_map/ppermute | solution.py:811
  48.3 6.8 %collective-permute-start.13 = (bf16[128,1024]{1,0:T(8,128)(2,1)S(1)}, bf16[128,1024]{1,0:T(8,128)(2,1)}, u32[]{:S(2)}, u32[]{:S(2)}) collective-permute-start(bf16[128,1024]{1,0:T(8,128)(2,1)S(1)} %collective-permute-done.4.refs_4_), channel_id=1, source_target_pairs={{0,2},{2,0},{4,6},{6,4},{8,10},{10,8},{12,14},{14,12},{16,18},{18,... | collective-permute-start | bytes 786440 | tf_op jit(solution)/shard_map/ppermute | solution.py:811
  48.3 6.8 %collective-permute-start.14 = (bf16[128,1024]{1,0:T(8,128)(2,1)S(1)}, bf16[128,1024]{1,0:T(8,128)(2,1)}, u32[]{:S(2)}, u32[]{:S(2)}) collective-permute-start(bf16[128,1024]{1,0:T(8,128)(2,1)S(1)} %collective-permute-done.5.refs_5_), channel_id=1, source_target_pairs={{0,2},{2,0},{4,6},{6,4},{8,10},{10,8},{12,14},{14,12},{16,18},{18,... | collective-permute-start | bytes 786440 | tf_op jit(solution)/shard_map/ppermute | solution.py:811
  48.8 6.3 %collective-permute-start.15 = (bf16[128,1024]{1,0:T(8,128)(2,1)S(1)}, bf16[128,1024]{1,0:T(8,128)(2,1)}, u32[]{:S(2)}, u32[]{:S(2)}) collective-permute-start(bf16[128,1024]{1,0:T(8,128)(2,1)S(1)} %collective-permute-done.6.refs_6_), channel_id=1, source_target_pairs={{0,2},{2,0},{4,6},{6,4},{8,10},{10,8},{12,14},{14,12},{16,18},{18,... | collective-permute-start | bytes 786440 | tf_op jit(solution)/shard_map/ppermute | solution.py:811
  48.9 6.2 %collective-permute-start.16 = (bf16[128,1024]{1,0:T(8,128)(2,1)S(1)}, bf16[128,1024]{1,0:T(8,128)(2,1)}, u32[]{:S(2)}, u32[]{:S(2)}) collective-permute-start(bf16[128,1024]{1,0:T(8,128)(2,1)S(1)} %constant_dynamic-update-slice_fusion.refs_7_), channel_id=1, source_target_pairs={{0,2},{2,0},{4,6},{6,4},{8,10},{10,8},{12,14},{14,12},{16,18},{18,... | collective-permute-start | bytes 786440 | tf_op jit(solution)/shard_map/ppermute | solution.py:811
  53.8 30.1 %collective-permute-start.17 = (bf16[256,1024]{1,0:T(8,128)(2,1)}, bf16[256,1024]{1,0:T(8,128)(2,1)}, u32[]{:S(2)}, u32[]{:S(2)}) collective-permute-start(bf16[256,1024]{1,0:T(8,128)(2,1)} %constant_dynamic-slice_fusion.3), channel_id=1, source_target_pairs={{0,1},{1,0},{2,3},{3,2},{4,5},{5,4},{6,7},{7,6},{8,9},{9,8},{10,11... | collective-permute-start | bytes 1572872 | tf_op jit(solution)/shard_map/ppermute | solution.py:835
  76.1 16.1 %all-to-all-start = ((bf16[16,64,128]{2,1,0:T(8,128)(2,1)}), bf16[16,64,128]{2,1,0:T(8,128)(2,1)}, u32[]{:S(2)}, u32[]{:S(2)}) async-start(bf16[16,64,128]{2,1,0:T(8,128)(2,1)} %copy-done.1), calls=%async_computation | async-start | bytes 524288 | tf_op jit(solution)/shard_map/all_to_all | solution.py:940
  83.9 9.6 %collective-permute-start.18 = (bf16[256,1024]{1,0:T(8,128)(2,1)}, bf16[256,1024]{1,0:T(8,128)(2,1)}, u32[]{:S(2)}, u32[]{:S(2)}) collective-permute-start(bf16[256,1024]{1,0:T(8,128)(2,1)} %collective-permute-done.17), channel_id=1, source_target_pairs={{0,2},{2,0},{4,6},{6,4},{8,10},{10,8},{12,14},{14,12},{16,18},{18,... | collective-permute-start | bytes 1572872 | tf_op jit(solution)/shard_map/ppermute | solution.py:811
  99.2 30.3 %all-to-all-start.1 = ((bf16[8,64,1024]{2,1,0:T(8,128)(2,1)}), bf16[8,64,1024]{2,1,0:T(8,128)(2,1)}, u32[]{:S(2)}, u32[]{:S(2)}) async-start(bf16[8,64,1024]{2,1,0:T(8,128)(2,1)} %bitcast.184), calls=%async_computation.1 | async-start | bytes 2097152 | tf_op jit(solution)/shard_map/all_to_all | solution.py:975
  103.5 65.7 %collective-permute-start.20 = (bf16[512,2816]{1,0:T(8,128)(2,1)}, bf16[512,2816]{1,0:T(8,128)(2,1)}, u32[]{:S(2)}, u32[]{:S(2)}) collective-permute-start(bf16[512,2816]{1,0:T(8,128)(2,1)} %bitcast.223), channel_id=1, source_target_pairs={{0,1},{1,0},{2,3},{3,2},{4,5},{5,4},{6,7},{7,6},{8,9},{9,8},{10,11... | collective-permute-start | bytes 8650760 | tf_op jit(solution)/shard_map/ppermute | solution.py:835
  129.5 30.3 %all-to-all-start.3 = ((bf16[8,64,1024]{2,1,0:T(8,128)(2,1)}), bf16[8,64,1024]{2,1,0:T(8,128)(2,1)}, u32[]{:S(2)}, u32[]{:S(2)}) async-start(bf16[8,64,1024]{2,1,0:T(8,128)(2,1)} %bitcast.193), calls=%async_computation.3 | async-start | bytes 2097152 | tf_op jit(solution)/shard_map/all_to_all | solution.py:975
  134.3 35.0 %collective-permute-start.19 = (bf16[512,1024]{1,0:T(8,128)(2,1)}, bf16[512,1024]{1,0:T(8,128)(2,1)}, u32[]{:S(2)}, u32[]{:S(2)}) collective-permute-start(bf16[512,1024]{1,0:T(8,128)(2,1)} %bitcast.24), channel_id=1, source_target_pairs={{0,2},{2,0},{4,6},{6,4},{8,10},{10,8},{12,14},{14,12},{16,18},{18,... | collective-permute-start | bytes 3145736 | tf_op jit(solution)/shard_map/ppermute | solution.py:811
  134.3 65.8 %collective-permute-start.21 = (bf16[512,1408]{1,0:T(8,128)(2,1)}, bf16[512,1408]{1,0:T(8,128)(2,1)}, u32[]{:S(2)}, u32[]{:S(2)}) collective-permute-start(bf16[512,1408]{1,0:T(8,128)(2,1)} %bitcast.226), channel_id=1, source_target_pairs={{0,1},{1,0},{2,3},{3,2},{4,5},{5,4},{6,7},{7,6},{8,9},{9,8},{10,11... | collective-permute-start | bytes 4325384 | tf_op jit(solution)/shard_map/ppermute | solution.py:835
  137.6 117.2 %collective-permute-start.25 = (bf16[256,3072]{1,0:T(8,128)(2,1)}, bf16[256,3072]{1,0:T(8,128)(2,1)}, u32[]{:S(2)}, u32[]{:S(2)}) collective-permute-start(bf16[256,3072]{1,0:T(8,128)(2,1)} %constant_dynamic-slice_fusion.2), channel_id=1, source_target_pairs={{0,1},{1,0},{2,3},{3,2},{4,5},{5,4},{6,7},{7,6},{8,9},{9,8},{10,11... | collective-permute-start | bytes 4718600 | tf_op jit(solution)/shard_map/ppermute | solution.py:835
  159.9 40.3 %collective-permute-start.23 = (bf16[512,1024]{1,0:T(8,128)(2,1)}, bf16[512,1024]{1,0:T(8,128)(2,1)S(1)}, u32[]{:S(2)}, u32[]{:S(2)}) collective-permute-start(bf16[512,1024]{1,0:T(8,128)(2,1)} %bitcast.37), channel_id=1, source_target_pairs={{0,2},{2,0},{4,6},{6,4},{8,10},{10,8},{12,14},{14,12},{16,18},{18,... | collective-permute-start | bytes 3145736 | tf_op jit(solution)/shard_map/ppermute | solution.py:811
  221.3 33.6 %collective-permute-start.22 = (bf16[512,1024]{1,0:T(8,128)(2,1)S(1)}, bf16[512,1024]{1,0:T(8,128)(2,1)S(1)}, u32[]{:S(2)}, u32[]{:S(2)}) collective-permute-start(bf16[512,1024]{1,0:T(8,128)(2,1)S(1)} %slice.335), channel_id=1, source_target_pairs={{0,2},{2,0},{4,6},{6,4},{8,10},{10,8},{12,14},{14,12},{16,18},{18,... | collective-permute-start | bytes 3145736 | tf_op jit(solution)/shard_map/ppermute | solution.py:811
  229.1 101.3 %collective-permute-start.45 = (bf16[512,2816]{1,0:T(8,128)(2,1)}, bf16[512,2816]{1,0:T(8,128)(2,1)}, u32[]{:S(2)}, u32[]{:S(2)}) collective-permute-start(bf16[512,2816]{1,0:T(8,128)(2,1)} %convolution_convert_fusion), channel_id=1, source_target_pairs={{0,1},{1,0},{2,3},{3,2},{4,5},{5,4},{6,7},{7,6},{8,9},{9,8},{10,11... | collective-permute-start | bytes 8650760 | tf_op jit(solution)/shard_map/ppermute | solution.py:835
  246.5 15.9 %collective-permute-start.24 = (bf16[512,1024]{1,0:T(8,128)(2,1)}, bf16[512,1024]{1,0:T(8,128)(2,1)}, u32[]{:S(2)}, u32[]{:S(2)}) collective-permute-start(bf16[512,1024]{1,0:T(8,128)(2,1)} %slice.334), channel_id=1, source_target_pairs={{0,2},{2,0},{4,6},{6,4},{8,10},{10,8},{12,14},{14,12},{16,18},{18,... | collective-permute-start | bytes 3145736 | tf_op jit(solution)/shard_map/ppermute | solution.py:811
  250.9 74.5 %collective-permute-start.46 = (bf16[512,1408]{1,0:T(8,128)(2,1)}, bf16[512,1408]{1,0:T(8,128)(2,1)}, u32[]{:S(2)}, u32[]{:S(2)}) collective-permute-start(bf16[512,1408]{1,0:T(8,128)(2,1)} %convolution_convert_fusion.1), channel_id=1, source_target_pairs={{0,1},{1,0},{2,3},{3,2},{4,5},{5,4},{6,7},{7,6},{8,9},{9,8},{10,11... | collective-permute-start | bytes 4325384 | tf_op jit(solution)/shard_map/ppermute | solution.py:835
  254.8 260.1 %collective-permute-start.26 = (bf16[256,3072]{1,0:T(8,128)(2,1)}, bf16[256,3072]{1,0:T(8,128)(2,1)}, u32[]{:S(2)}, u32[]{:S(2)}) collective-permute-start(bf16[256,3072]{1,0:T(8,128)(2,1)} %collective-permute-done.25), channel_id=1, source_target_pairs={{0,2},{2,0},{4,6},{6,4},{8,10},{10,8},{12,14},{14,12},{16,18},{18,... | collective-permute-start | bytes 4718600 | tf_op jit(solution)/shard_map/ppermute | solution.py:811
  256.2 85.4 %all-to-all-start.2 = ((bf16[8,64,1024]{2,1,0:T(8,128)(2,1)}), bf16[8,64,1024]{2,1,0:T(8,128)(2,1)}, u32[]{:S(2)}, u32[]{:S(2)}) async-start(bf16[8,64,1024]{2,1,0:T(8,128)(2,1)} %bitcast.186), calls=%async_computation.2 | async-start | bytes 2097152 | tf_op jit(solution)/shard_map/all_to_all | solution.py:975
  341.6 31.5 %all-to-all-start.4 = ((bf16[8,64,1024]{2,1,0:T(8,128)(2,1)}), bf16[8,64,1024]{2,1,0:T(8,128)(2,1)}, u32[]{:S(2)}, u32[]{:S(2)}) async-start(bf16[8,64,1024]{2,1,0:T(8,128)(2,1)} %bitcast.185), calls=%async_computation.4 | async-start | bytes 2097152 | tf_op jit(solution)/shard_map/all_to_all | solution.py:975
  382.9 4.1 collective-permute-start.48
  387.0 4.1 collective-permute-start.49
  391.1 7.7 %collective-permute-start.50 = (f32[80,128]{1,0:T(8,128)S(1)}, f32[80,128]{1,0:T(8,128)S(1)}, u32[]{:S(2)}, u32[]{:S(2)}) collective-permute-start(f32[80,128]{1,0:T(8,128)S(1)} %add.227), channel_id=1, source_target_pairs={{0,16},{2,18},{4,20},{6,22},{8,24},{10,26},{12,28},{14,30},{16,0},... | collective-permute-start | bytes 122888 | tf_op jit(solution)/shard_map/ppermute | solution.py:841
  393.7 15.3 %all-to-all-start.5 = ((bf16[16,64,128]{2,1,0:T(8,128)(2,1)}), bf16[16,64,128]{2,1,0:T(8,128)(2,1)}, u32[]{:S(2)}, u32[]{:S(2)}) async-start(bf16[16,64,128]{2,1,0:T(8,128)(2,1)} %bitcast.194), calls=%async_computation.5 | async-start | bytes 524288 | tf_op jit(solution)/shard_map/all_to_all | solution.py:1049
  398.9 4.5 collective-permute-start.51
  401.5 51.6 %collective-permute-start.44 = (bf16[512,1024]{1,0:T(8,128)(2,1)}, bf16[512,1024]{1,0:T(8,128)(2,1)}, u32[]{:S(2)}, u32[]{:S(2)}) collective-permute-start(bf16[512,1024]{1,0:T(8,128)(2,1)} %convolution_convert_fusion.2), channel_id=1, source_target_pairs={{0,1},{1,0},{2,3},{3,2},{4,5},{5,4},{6,7},{7,6},{8,9},{9,8},{10,11... | collective-permute-start | bytes 3145736 | tf_op jit(solution)/shard_map/ppermute | solution.py:835
  434.0 6.7 %collective-permute-start.27 = (bf16[192,512]{1,0:T(8,128)(2,1)S(1)}, bf16[192,512]{1,0:T(8,128)(2,1)S(1)}, u32[]{:S(2)}, u32[]{:S(2)}) collective-permute-start(bf16[192,512]{1,0:T(8,128)(2,1)S(1)} %select_convert_fusion), channel_id=1, source_target_pairs={{0,1},{1,0},{2,3},{3,2},{4,5},{5,4},{6,7},{7,6},{8,9},{9,8},{10,11... | collective-permute-start | bytes 589832 | tf_op jit(solution)/shard_map/ppermute | solution.py:835
  441.5 8.2 %collective-permute-start.28 = (bf16[192,512]{1,0:T(8,128)(2,1)S(1)}, bf16[192,512]{1,0:T(8,128)(2,1)S(1)}, u32[]{:S(2)}, u32[]{:S(2)}) collective-permute-start(bf16[192,512]{1,0:T(8,128)(2,1)S(1)} %get-tuple-element.65), channel_id=1, source_target_pairs={{0,8},{2,10},{8,16},{10,18},{16,24},{18,26},{24,28},{26,30},{28,20... | collective-permute-start | bytes 589832 | tf_op jit(solution)/shard_map/ppermute | solution.py:817
  442.9 8.6 %collective-permute-start.29 = (bf16[192,512]{1,0:T(8,128)(2,1)S(1)}, bf16[192,512]{1,0:T(8,128)(2,1)S(1)}, u32[]{:S(2)}, u32[]{:S(2)}) collective-permute-start(bf16[192,512]{1,0:T(8,128)(2,1)S(1)} %get-tuple-element.65), channel_id=1, source_target_pairs={{0,4},{2,6},{8,0},{10,2},{16,8},{18,10},{24,16},{26,18},{28,24},{3... | collective-permute-start | bytes 589832 | tf_op jit(solution)/shard_map/ppermute | solution.py:818
  443.8 68.0 %all-to-all-start.6 = ((bf16[16,192,128]{2,1,0:T(8,128)(2,1)}), bf16[16,192,128]{2,1,0:T(8,128)(2,1)S(1)}, u32[]{:S(2)}, u32[]{:S(2)}) async-start(bf16[16,192,128]{2,1,0:T(8,128)(2,1)} %get-tuple-element.24), calls=%async_computation.6 | async-start | bytes 1572864 | tf_op jit(solution)/shard_map/all_to_all | solution.py:1063
  449.2 103.1 %all-reduce.12.cloned.1.call-start = ((), (), s32[]{:S(2)}) async-start(), calls=%async_computation.7 | async-start | bytes 2097152 | tf_op jit(solution)/shard_map/psum | solution.py:1058
  449.3 56.4 %collective-permute-start.36 = (bf16[192,512]{1,0:T(8,128)(2,1)S(1)}, bf16[192,512]{1,0:T(8,128)(2,1)S(1)}, u32[]{:S(2)}, u32[]{:S(2)}) collective-permute-start(bf16[192,512]{1,0:T(8,128)(2,1)S(1)} %get-tuple-element.65), channel_id=1, source_target_pairs={{0,2},{2,0},{4,6},{6,4},{8,10},{10,8},{12,14},{14,12},{16,18},{18,... | collective-permute-start | bytes 589832 | tf_op jit(solution)/shard_map/ppermute | solution.py:811
  449.7 19.2 %collective-permute-start.30 = (bf16[192,512]{1,0:T(8,128)(2,1)S(1)}, bf16[192,512]{1,0:T(8,128)(2,1)S(1)}, u32[]{:S(2)}, u32[]{:S(2)}) collective-permute-start(bf16[192,512]{1,0:T(8,128)(2,1)S(1)} %collective-permute-done.28), channel_id=1, source_target_pairs={{0,8},{2,10},{8,16},{10,18},{16,24},{18,26},{24,28},{26,30},{28,20... | collective-permute-start | bytes 589832 | tf_op jit(solution)/shard_map/ppermute | solution.py:817
  451.4 19.9 %collective-permute-start.31 = (bf16[192,512]{1,0:T(8,128)(2,1)S(1)}, bf16[192,512]{1,0:T(8,128)(2,1)S(1)}, u32[]{:S(2)}, u32[]{:S(2)}) collective-permute-start(bf16[192,512]{1,0:T(8,128)(2,1)S(1)} %collective-permute-done.29), channel_id=1, source_target_pairs={{0,4},{2,6},{8,0},{10,2},{16,8},{18,10},{24,16},{26,18},{28,24},{3... | collective-permute-start | bytes 589832 | tf_op jit(solution)/shard_map/ppermute | solution.py:818
  453.1 53.7 %collective-permute-start.37 = (bf16[192,512]{1,0:T(8,128)(2,1)S(1)}, bf16[192,512]{1,0:T(8,128)(2,1)}, u32[]{:S(2)}, u32[]{:S(2)}) collective-permute-start(bf16[192,512]{1,0:T(8,128)(2,1)S(1)} %collective-permute-done.28), channel_id=1, source_target_pairs={{0,2},{2,0},{4,6},{6,4},{8,10},{10,8},{12,14},{14,12},{16,18},{18,... | collective-permute-start | bytes 589832 | tf_op jit(solution)/shard_map/ppermute | solution.py:811
  469.0 39.5 %collective-permute-start.38 = (bf16[192,512]{1,0:T(8,128)(2,1)S(1)}, bf16[192,512]{1,0:T(8,128)(2,1)S(1)}, u32[]{:S(2)}, u32[]{:S(2)}) collective-permute-start(bf16[192,512]{1,0:T(8,128)(2,1)S(1)} %collective-permute-done.29), channel_id=1, source_target_pairs={{0,2},{2,0},{4,6},{6,4},{8,10},{10,8},{12,14},{14,12},{16,18},{18,... | collective-permute-start | bytes 589832 | tf_op jit(solution)/shard_map/ppermute | solution.py:811
  471.4 13.3 %collective-permute-start.32 = (bf16[192,512]{1,0:T(8,128)(2,1)S(1)}, bf16[192,512]{1,0:T(8,128)(2,1)S(1)}, u32[]{:S(2)}, u32[]{:S(2)}) collective-permute-start(bf16[192,512]{1,0:T(8,128)(2,1)S(1)} %collective-permute-done.30), channel_id=1, source_target_pairs={{0,8},{2,10},{8,16},{10,18},{16,24},{18,26},{24,28},{26,30},{28,20... | collective-permute-start | bytes 589832 | tf_op jit(solution)/shard_map/ppermute | solution.py:817
  484.7 8.8 %collective-permute-start.33 = (bf16[192,512]{1,0:T(8,128)(2,1)S(1)}, bf16[192,512]{1,0:T(8,128)(2,1)S(1)}, u32[]{:S(2)}, u32[]{:S(2)}) collective-permute-start(bf16[192,512]{1,0:T(8,128)(2,1)S(1)} %collective-permute-done.31), channel_id=1, source_target_pairs={{0,4},{2,6},{8,0},{10,2},{16,8},{18,10},{24,16},{26,18},{28,24},{3... | collective-permute-start | bytes 589832 | tf_op jit(solution)/shard_map/ppermute | solution.py:818
  493.5 5.0 collective-permute-start.34
  498.5 4.9 collective-permute-start.35
  503.4 6.3 %collective-permute-start.39 = (bf16[192,512]{1,0:T(8,128)(2,1)S(1)}, bf16[192,512]{1,0:T(8,128)(2,1)S(1)}, u32[]{:S(2)}, u32[]{:S(2)}) collective-permute-start(bf16[192,512]{1,0:T(8,128)(2,1)S(1)} %collective-permute-done.30), channel_id=1, source_target_pairs={{0,2},{2,0},{4,6},{6,4},{8,10},{10,8},{12,14},{14,12},{16,18},{18,... | collective-permute-start | bytes 589832 | tf_op jit(solution)/shard_map/ppermute | solution.py:811
  505.6 4.7 collective-permute-start.40
  506.8 4.2 collective-permute-start.41
  508.5 10.8 %collective-permute-start.42 = (bf16[192,512]{1,0:T(8,128)(2,1)S(1)}, bf16[192,512]{1,0:T(8,128)(2,1)}, u32[]{:S(2)}, u32[]{:S(2)}) collective-permute-start(bf16[192,512]{1,0:T(8,128)(2,1)S(1)} %collective-permute-done.33), channel_id=1, source_target_pairs={{0,2},{2,0},{4,6},{6,4},{8,10},{10,8},{12,14},{14,12},{16,18},{18,... | collective-permute-start | bytes 589832 | tf_op jit(solution)/shard_map/ppermute | solution.py:811
  509.7 13.3 %collective-permute-start.43 = (bf16[192,512]{1,0:T(8,128)(2,1)}, bf16[192,512]{1,0:T(8,128)(2,1)}, u32[]{:S(2)}, u32[]{:S(2)}) collective-permute-start(bf16[192,512]{1,0:T(8,128)(2,1)} %constant_dynamic-update-slice_fusion.2), channel_id=1, source_target_pairs={{0,2},{2,0},{4,6},{6,4},{8,10},{10,8},{12,14},{14,12},{16,18},{18,... | collective-permute-start | bytes 589832 | tf_op jit(solution)/shard_map/ppermute | solution.py:811
  518.7 2.2 collective-permute-start.52
  520.9 8.0 %collective-permute-start.53 = (f32[16,128]{1,0:T(8,128)S(1)}, f32[16,128]{1,0:T(8,128)S(1)}, u32[]{:S(2)}, u32[]{:S(2)}) collective-permute-start(f32[16,128]{1,0:T(8,128)S(1)} %fusion.113), channel_id=1, source_target_pairs={{0,4},{2,6},{4,0},{6,2},{8,12},{10,14},{12,8},{14,10},{16,20},{18,... | collective-permute-start | bytes 24584 | tf_op jit(solution)/shard_map/ppermute | solution.py:841
  529.0 26.2 %collective-permute-start.54 = (f32[16,128]{1,0:T(8,128)S(1)}, f32[16,128]{1,0:T(8,128)S(1)}, u32[]{:S(2)}, u32[]{:S(2)}) collective-permute-start(f32[16,128]{1,0:T(8,128)S(1)} %fusion.144), channel_id=1, source_target_pairs={{0,8},{2,10},{4,12},{6,14},{8,0},{10,2},{12,4},{14,6},{16,24},{18,... | collective-permute-start | bytes 24584 | tf_op jit(solution)/shard_map/ppermute | solution.py:841
  555.2 4.6 collective-permute-start.55
  559.7 3.7 collective-permute-start.56
  (52 other events, 704.1 us)
Sparse Core Ops, SparseCore 0:
  455.9 96.3 all-reduce.11
